TPU v7x, 256 devices: a whole 4x4x8 slice. The times are simulated.
256 devices in a mesh: grid: 16 (over z_hi, y), space: 16 (over z_lo, x, core).
Axes of the slice: x: 4, y: 4, z: 8 (z_hi: 4, z_lo: 2; z = z_hi * 2 + z_lo), core: 2. Of those that a mesh axis runs over, the one named last changes fastest.
Arguments:
- density: float32 [16, 512, 64, 128], P('grid', 'space'), may hold values from -6 to 6
- kappa: float32 [16, 512, 64, 128], P('grid', 'space'), may hold values from 0.02 to 0.16
- levels: int32 [16, 3], P('grid'), may hold values from 3 to 6, as said below
- coefs: int32 [16], P('grid'), may hold values from -2 to 1, as said below
Outputs:
- combined: float32 [16, 512, 64, 128], P('grid', 'space')
Inputs may be any that keep to these rules, and one draw needn't show every extreme that they name: `levels`: each level vector is (3, 3, 3) plus nonnegative integers summing to 1, 2 or 3, no two grids alike; a level at or above log2 of an axis's cells keeps that whole axis. coefs[g] is +1 where the grid's levels sum to 12 or 10 and -2 where they sum to 11.
All inputs are finite; a program needn't handle non-finite values.
Results may differ from a plain program's by a relative error of at most 0.0003.
Values sent between devices are 32-bit elements; how exact they have to be, the bound alone decides.
No kernel may reach another device: no remote copies, remote signals or barrier semaphores. Data moves between devices by JAX's collectives and lax.ppermute only.
A program may use at most 64 MiB of HBM per device.

v0:
```python
import functools

import jax
import jax.numpy as jnp
import numpy as np
from jax import lax
from jax.experimental import pallas as pl
from jax.experimental.pallas import tpu as pltpu
from jax.sharding import PartitionSpec as P

ITERS = 8
LOW = 3
SPAN = 3
ROWS = 32
GAP = 8
NODES = ROWS // GAP + 1
LEFT = ITERS
RIGHT = ITERS + 1
TALL = LEFT + ROWS + RIGHT
NY = 64
NZ = 128
TOP = 1 << (LOW + SPAN)


def level_order(count):
    step = count >> (LOW + SPAN)
    order = list(range(0, count, count >> LOW))
    for level in range(LOW + 1, LOW + SPAN + 1):
        gap = count >> level
        order += list(range(gap, count, 2 * gap))
    assert len(order) == TOP and all(i % step == 0 for i in order)
    return order


def tables(count):
    order = level_order(count)
    hier = np.eye(count)
    hats = np.eye(count)
    for index in range(1, count):
        gap = index & -index
        hier[index, (index - gap) % count] -= 0.5
        hier[index, (index + gap) % count] -= 0.5
    gap = count // 2
    while gap:
        for index in range(gap, count, 2 * gap):
            hats[index] += 0.5 * (hats[(index - gap) % count] + hats[(index + gap) % count])
        gap //= 2
    return hier[order], hats[:, order]


@functools.lru_cache(None)
def constants():
    hy, dy = tables(NY)
    hz, dz = tables(NZ)
    spread = [v + 8 * s for v in range(8) for s in range(8)]
    hy = hy[:, spread]
    hz_t = np.zeros((NZ, 128))
    hz_t[:, :TOP] = hz.T
    dz_t = np.zeros((128, NZ))
    dz_t[:TOP] = dz.T
    hy3 = np.concatenate([hy] * 3, axis=1)
    dy3 = np.concatenate([dy] * 3, axis=1)
    return tuple(np.asarray(m, np.float32) for m in (hy3, hz_t, dy3, dz_t))


def staircase():
    widths = {0: SPAN, 1: SPAN - 1, 2: SPAN - 2, 3: SPAN - 3, 4: SPAN - 3}
    blocks = []
    place = 0
    for plane, left in widths.items():
        for extra in range(left + 1):
            groups = range(1 << (extra - 1), 1 << extra) if extra else range(1)
            for group in groups:
                width = 1 << (LOW + left - extra)
                blocks.append((plane, group, width, place // 128, place % 128))
                assert place % 128 + width <= 128
                place += width
    return blocks, -(-place // 128)


BLOCKS, TILES = staircase()
SHARED = 1 + max(b[3] for b in BLOCKS if b[0] < 2)


def split3(x):
    hi = x.astype(jnp.bfloat16)
    rest = x - hi.astype(jnp.float32)
    mid = rest.astype(jnp.bfloat16)
    lo = (rest - mid.astype(jnp.float32)).astype(jnp.bfloat16)
    return hi, mid, lo


def rows_dot(weights3, plane):
    stacked = jnp.concatenate(split3(plane), axis=0)
    return jnp.dot(weights3, stacked, preferred_element_type=jnp.float32)


def lanes_dot(planes, weights):
    total = None
    for piece in split3(planes):
        part = jnp.dot(piece, weights, preferred_element_type=jnp.float32)
        total = part if total is None else total + part
    return total


def next_y(row):
    return jnp.concatenate([row[1:], pltpu.roll(row[0:1], 7, 1)], axis=0)


def prev_y(row):
    return jnp.concatenate([pltpu.roll(row[7:8], 1, 1), row[:7]], axis=0)


def next_z(row):
    return pltpu.roll(row, NZ - 1, 2)


def prev_z(row):
    return pltpu.roll(row, 1, 2)


def fetch(ref, index):
    return jnp.stack([ref[index, pl.ds(v, 8, 8), :] for v in range(8)], axis=0)


def advance(f_ref, cx_ref, cy_ref, cz_ref, start, count):
    def one(i, here, flux):
        after = f_ref[i + 1]
        flux_x = cx_ref[i] * (after - here)
        flux_y = cy_ref[i] * (next_y(here) - here)
        flux_z = cz_ref[i] * (next_z(here) - here)
        f_ref[i] = (here + (flux_x - flux)) + ((flux_y - prev_y(flux_y)) + (flux_z - prev_z(flux_z)))
        return after, flux_x

    before = f_ref[start - 1]
    here = f_ref[start]
    flux = cx_ref[start - 1] * (here - before)
    unroll = 4

    def body(t, carry):
        here, flux = carry
        for k in range(unroll):
            here, flux = one(start + t * unroll + k, here, flux)
        return here, flux

    whole = count // unroll
    if whole:
        here, flux = lax.fori_loop(0, whole, body, (here, flux))
    for k in range(whole * unroll, count):
        here, flux = one(start + k, here, flux)


def diffuse_kernel(lev, coef, odd, den, kap, left, right, hy3, hz, out, f_ref, cx_ref, cy_ref, cz_ref):
    def load_rows(f_src, f_base, k_src, k_base, count, base, carry):
        def body(t, before):
            k = fetch(k_src, k_base + t)
            f_ref[base + t] = fetch(f_src, f_base + t)
            cx_ref[jnp.maximum(base + t - 1, 0)] = 0.5 * (before + k)
            cy_ref[base + t] = 0.5 * (k + next_y(k))
            cz_ref[base + t] = 0.5 * (k + next_z(k))
            return k
        return lax.fori_loop(0, count, body, carry)

    k = jnp.zeros((8, 8, 128), jnp.float32)
    k = load_rows(left, 0, left, LEFT, LEFT, 0, k)
    k = load_rows(den, 0, kap, 0, ROWS, LEFT, k)
    k = load_rows(right, 0, right, RIGHT, RIGHT, LEFT + ROWS, k)

    for step in range(1, ITERS + 1):
        reach = ITERS - step
        if 2 * reach + 1 >= GAP:
            advance(f_ref, cx_ref, cy_ref, cz_ref, LEFT - reach, ROWS + 2 * reach + 1)
        else:
            def node(n, _, reach=reach):
                advance(f_ref, cx_ref, cy_ref, cz_ref, LEFT + n * GAP - reach, 2 * reach + 1)
                return 0
            lax.fori_loop(0, NODES, node, 0)

    planes = []
    for n in range(NODES):
        plane = f_ref[LEFT + n * GAP].reshape(NY, NZ)
        planes.append(rows_dot(hy3[...], plane))
    nodal = lanes_dot(jnp.concatenate(planes, axis=0), hz[...]).reshape(NODES, 8, 8, 128)

    level_x, level_y, level_z = lev[0, 0], lev[0, 1], lev[0, 2]
    weight = coef[0].astype(jnp.float32)
    swapped = odd[0] == 1
    lane = lax.broadcasted_iota(jnp.int32, (8, 128), 1)
    groups_y = lax.shift_left(1, level_y - LOW)
    width_z = lax.shift_left(1, level_z)

    def planes_of(group):
        u = [nodal[n, group] for n in range(NODES)]
        outer = jnp.where(swapped, u[4], u[0])
        inner = jnp.where(swapped, u[0], u[4])
        return (
            outer,
            0.5 * (inner - outer),
            u[2] - 0.5 * (u[0] + u[4]),
            u[1] - 0.5 * (u[0] + u[2]),
            u[3] - 0.5 * (u[2] + u[4]),
        )

    need = (LOW, LOW + 1, LOW + 2, LOW + 3, LOW + 3)
    cache = {}
    tiles = [jnp.zeros((8, 128), jnp.float32)] * TILES
    for plane, group, width, tile, first in BLOCKS:
        if group not in cache:
            cache[group] = planes_of(group)
        keep = (lane < jnp.minimum(width_z, width)) & (group < groups_y) & (level_x >= need[plane])
        value = jnp.where(keep, weight * cache[group][plane], 0.0)
        tiles[tile] = tiles[tile] + (pltpu.roll(value, first, 1) if first else value)
    for member in range(out.shape[0]):
        for tile in range(TILES):
            out[member, 8 * tile : 8 * tile + 8] = tiles[tile]


def spread_kernel(lev, odd, mine, other, dy3, dz, out):
    level_x, level_y, level_z = lev[0, 0], lev[0, 1], lev[0, 2]
    swapped = odd[0] == 1
    lane = lax.broadcasted_iota(jnp.int32, (8, 128), 1)
    groups_y = lax.shift_left(1, level_y - LOW)
    width_z = lax.shift_left(1, level_z)
    need = (LOW, LOW + 1, LOW + 2, LOW + 3, LOW + 3)
    own = [mine[8 * t : 8 * t + 8] for t in range(TILES)]
    theirs = [other[8 * t : 8 * t + 8] for t in range(SHARED)]
    zero = jnp.zeros((8, 128), jnp.float32)
    planes = [[zero] * 8 for _ in range(5)]
    outer_other = [zero] * 8
    for plane, group, width, tile, first in BLOCKS:
        keep = (lane < jnp.minimum(width_z, width)) & (group < groups_y) & (level_x >= need[plane])

        def pick(source):
            value = pltpu.roll(source, 128 - first, 1) if first else source
            return jnp.where(keep, value, 0.0)

        if plane == 0:
            planes[0][group] = pick(own[tile])
            outer_other[group] = pick(theirs[tile])
        elif plane == 1:
            planes[1][group] = pick(own[tile] + theirs[tile])
        else:
            planes[plane][group] = pick(own[tile])
    wide = []
    outer = jnp.concatenate(planes[0], axis=0)
    middle = 0.5 * (outer + jnp.concatenate(outer_other, axis=0)) + jnp.concatenate(planes[1], axis=0)
    n0 = jnp.where(swapped, middle, outer)
    n4 = jnp.where(swapped, outer, middle)
    n2 = 0.5 * (n0 + n4) + jnp.concatenate(planes[2], axis=0)
    n1 = 0.5 * (n0 + n2) + jnp.concatenate(planes[3], axis=0)
    n3 = 0.5 * (n2 + n4) + jnp.concatenate(planes[4], axis=0)
    for n in (n0, n1, n2, n3, n4):
        wide.append(rows_dot(dy3[...], n))
    full = lanes_dot(jnp.concatenate(wide, axis=0), dz[...]).reshape(NODES, NY, NZ)
    for q in range(NODES - 1):
        slope = (full[q + 1] - full[q]) * (1.0 / GAP)
        for k in range(GAP):
            out[q * GAP + k] = full[q] + float(k) * slope


VMEM = pl.BlockSpec(memory_space=pltpu.VMEM)
SMEM = pl.BlockSpec(memory_space=pltpu.SMEM)


def diffuse(members, levels, coefs, odd, den, kap, left, right, interpret=False):
    hy3, hz, _, _ = constants()
    work = pltpu.VMEM((TALL, 8, 8, 128), jnp.float32)
    return pl.pallas_call(
        diffuse_kernel,
        out_shape=jax.ShapeDtypeStruct((members, 8 * TILES, 128), jnp.float32),
        in_specs=[SMEM] * 3 + [VMEM] * 6,
        out_specs=VMEM,
        scratch_shapes=[work] * 4,
        interpret=interpret,
        name="diffuse",
    )(levels, coefs, odd, den, kap, left, right, jnp.asarray(hy3, jnp.bfloat16), jnp.asarray(hz, jnp.bfloat16))


def spread(levels, odd, mine, other, interpret=False):
    _, _, dy3, dz = constants()
    return pl.pallas_call(
        spread_kernel,
        out_shape=jax.ShapeDtypeStruct((ROWS, NY, NZ), jnp.float32),
        in_specs=[SMEM] * 2 + [VMEM] * 4,
        out_specs=VMEM,
        interpret=interpret,
        name="spread",
    )(levels, odd, mine, other, jnp.asarray(dy3, jnp.bfloat16), jnp.asarray(dz, jnp.bfloat16))


def local(density, kappa, levels, coefs):
    den, kap = density[0], kappa[0]
    space, grid = lax.axis_size("space"), lax.axis_size("grid")
    assert den.shape == (ROWS, NY, NZ) and space * ROWS == 512
    up = [(i, (i + 1) % space) for i in range(space)]
    down = [(j, i) for i, j in up]
    pair = [(i, i ^ 1) for i in range(space)]
    left = lax.ppermute(jnp.concatenate([den[ROWS - LEFT :], kap[ROWS - LEFT :]], axis=0), "space", up)
    right = lax.ppermute(jnp.concatenate([den[:RIGHT], kap[:RIGHT]], axis=0), "space", down)
    odd = (lax.axis_index("space") % 2).astype(jnp.int32)[None]
    sent = diffuse(grid, levels, coefs, odd, den, kap, left, right)
    got = lax.all_to_all(sent, "grid", split_axis=0, concat_axis=0, tiled=True)
    total = jnp.sum(got, axis=0)
    other = lax.ppermute(total[: 8 * SHARED], "space", pair)
    return spread(levels, odd, total, other)[None]


def solution(mesh):
    in_specs = (
        P("grid", "space", None, None),
        P("grid", "space", None, None),
        P("grid", None),
        P("grid"),
    )
    out_specs = P("grid", "space", None, None)
    return jax.shard_map(local, mesh=mesh, in_specs=in_specs, out_specs=out_specs, check_vma=False)
```

profile of v0, /device:TPU:1, one launch (start us, length us, event | category | flops | bytes accessed | tf_op | source)
XLA Modules:
  0.0 62.9 jit_solution(16050028815237481243)
XLA Ops:
  0.0 1.1 %slice_bitcast_fusion = (f32[9,64,128]{2,1,0:T(8,128)S(1)}, f32[9,64,128]{2,1,0:T(8,128)S(1)}) fusion(f32[1,32,64,128]{3,2,1,0:T(8,128)} %param.9, f32[1,32,64,128]{3,2,1,0:T(8,128)} %param.8), kind=kLoop, calls=%fused_computation.2 | loop fusion | bytes 1179648 | tf_op jit(solution)/shard_map/slice | solution.py:299
  1.1 3.3 %collective-permute-start.1 = (f32[18,64,128]{2,1,0:T(8,128)S(1)}, f32[18,64,128]{2,1,0:T(8,128)S(1)}, u32[]{:S(2)}, u32[]{:S(2)}) collective-permute-start(f32[18,64,128]{2,1,0:T(8,128)S(1)} %pad_maximum_fusion), channel_id=1, source_target_pairs={{1,0},{2,1},{3,2},{4,3},{5,4},{6,5},{7,6},{8,7},{9,8},{10,9},{11,1... | collective-permute-start | bytes 1769480 | tf_op jit(solution)/shard_map/ppermute | solution.py:299
  4.4 1.1 %slice_bitcast_fusion.2 = (f32[8,64,128]{2,1,0:T(8,128)S(1)}, f32[8,64,128]{2,1,0:T(8,128)S(1)}) fusion(f32[1,32,64,128]{3,2,1,0:T(8,128)} %param.9, f32[1,32,64,128]{3,2,1,0:T(8,128)} %param.8), kind=kLoop, calls=%fused_computation.4 | loop fusion | bytes 1048576 | tf_op jit(solution)/shard_map/slice | solution.py:298
  5.5 0.1 collective-permute-start
  6.3 5.5 %collective-permute-done.left = f32[16,64,128]{2,1,0:T(8,128)S(1)} collective-permute-done((f32[16,64,128]{2,1,0:T(8,128)S(1)}, f32[16,64,128]{2,1,0:T(8,128)S(1)}, u32[]{:S(2)}, u32[]{:S(2)}) %collective-permute-start) | collective-permute-done | bytes 524320 | tf_op jit(solution)/shard_map/ppermute | solution.py:298
  11.8 0.0 copy-start.1
  11.8 0.0 collective-permute-done.1.right
  11.8 0.0 copy-start
  11.8 0.8 %copy-done.1 = f32[16,64,128]{2,1,0:T(8,128)} copy-done((f32[16,64,128]{2,1,0:T(8,128)}, f32[16,64,128]{2,1,0:T(8,128)S(1)}, u32[]{:S(2)}) %copy-start.1) | copy-done | bytes 524312
  12.5 0.2 copy-done
  12.7 18.7 %diffuse.1 = f32[16,24,128]{2,1,0:T(8,128)} custom-call(s32[1,3]{1,0:T(1,128)} %lev.3, s32[1]{0:T(128)S(6)} %copy.9.coef, s32[1]{0:T(128)} %bitcast.odd, f32[32,64,128]{2,1,0:T(8,128)} %bitcast.12, f32[32,64,128]{2,1,0:T(8,128)} %bitcast.13, f32[16,64,128]{2,1,0:T(8,128)} %copy-done.1, f32[18,64,128]{2,1,0:T(8,128)} %copy-done, ...), custom_call_target="tpu_custom_call" | custom-call | tf_op jit(solution)/shard_map/diffuse/pallas_call | solution.py:268
  31.5 20.3 %all_to_all.5 = f32[16,24,128]{2,1,0:T(8,128)S(1)} all-to-all(f32[16,24,128]{2,1,0:T(8,128)} %diffuse.1), channel_id=1, replica_groups=mesh['grid'=16,'space'=16] {'grid'}, dimensions={0} | all-to-all | bytes 393216 | tf_op jit(solution)/shard_map/all_to_all | solution.py:302
  51.8 0.0 copy-start.2
  51.8 7.3 %collective-permute-start.2 = (f32[16,128]{1,0:T(8,128)S(1)}, f32[16,128]{1,0:T(8,128)S(1)}, u32[]{:S(2)}, u32[]{:S(2)}) collective-permute-start(f32[16,128]{1,0:T(8,128)S(1)} %slice.36), channel_id=1, source_target_pairs={{0,1},{1,0},{2,3},{3,2},{4,5},{5,4},{6,7},{7,6},{8,9},{9,8},{10,11... | collective-permute-start | bytes 24584 | tf_op jit(solution)/shard_map/ppermute | solution.py:304
  59.1 0.8 %collective-permute-done.2.other = f32[16,128]{1,0:T(8,128)S(1)} collective-permute-done((f32[16,128]{1,0:T(8,128)S(1)}, f32[16,128]{1,0:T(8,128)S(1)}, u32[]{:S(2)}, u32[]{:S(2)}) %collective-permute-start.2) | collective-permute-done | bytes 8224 | tf_op jit(solution)/shard_map/ppermute | solution.py:304
  60.0 0.0 copy-done.2
  60.0 0.0 copy-start.3
  60.0 0.6 copy-done.3
  60.6 2.3 %spread.1 = f32[32,64,128]{2,1,0:T(8,128)} custom-call(s32[1,3]{1,0:T(1,128)} %lev.3, s32[1]{0:T(128)} %bitcast.odd, f32[24,128]{1,0:T(8,128)} %copy-done.2, f32[16,128]{1,0:T(8,128)} %copy-done.3, bf16[64,192]{1,0:T(8,128)(2,1)} %constant.29.clone.dy3, bf16[128,128]{1,0:T(8,128)(2,1)} %constant.30.clone.dz), custom_call_target="tpu_custom_call" | custom-call | tf_op jit(solution)/shard_map/spread/pallas_call | solution.py:281
  (4 shorter events, 0.1 us)
Async XLA Ops:
  1.1 10.6 %collective-permute-start.1 = (f32[18,64,128]{2,1,0:T(8,128)S(1)}, f32[18,64,128]{2,1,0:T(8,128)S(1)}, u32[]{:S(2)}, u32[]{:S(2)}) collective-permute-start(f32[18,64,128]{2,1,0:T(8,128)S(1)} %pad_maximum_fusion), channel_id=1, source_target_pairs={{1,0},{2,1},{3,2},{4,3},{5,4},{6,5},{7,6},{8,7},{9,8},{10,9},{11,1... | collective-permute-start | bytes 1769480 | tf_op jit(solution)/shard_map/ppermute | solution.py:299
  5.5 6.2 %collective-permute-start = (f32[16,64,128]{2,1,0:T(8,128)S(1)}, f32[16,64,128]{2,1,0:T(8,128)S(1)}, u32[]{:S(2)}, u32[]{:S(2)}) collective-permute-start(f32[16,64,128]{2,1,0:T(8,128)S(1)} %pad_maximum_fusion.1), channel_id=1, source_target_pairs={{0,1},{1,2},{2,3},{3,4},{4,5},{5,6},{6,7},{7,8},{8,9},{9,10},{10,1... | collective-permute-start | bytes 1572872 | tf_op jit(solution)/shard_map/ppermute | solution.py:298
  11.8 0.8 %copy-start.1 = (f32[16,64,128]{2,1,0:T(8,128)}, f32[16,64,128]{2,1,0:T(8,128)S(1)}, u32[]{:S(2)}) copy-start(f32[16,64,128]{2,1,0:T(8,128)S(1)} %collective-permute-done.left) | copy-start | bytes 1572868
  11.8 1.0 %copy-start = (f32[18,64,128]{2,1,0:T(8,128)}, f32[18,64,128]{2,1,0:T(8,128)S(1)}, u32[]{:S(2)}) copy-start(f32[18,64,128]{2,1,0:T(8,128)S(1)} %collective-permute-done.1.right) | copy-start | bytes 1769476
  51.8 8.1 %copy-start.2 = (f32[24,128]{1,0:T(8,128)}, f32[24,128]{1,0:T(8,128)S(1)}, u32[]{:S(2)}) copy-start(f32[24,128]{1,0:T(8,128)S(1)} %reduce_sum.9.mine) | copy-start | bytes 36868
  51.8 8.1 %collective-permute-start.2 = (f32[16,128]{1,0:T(8,128)S(1)}, f32[16,128]{1,0:T(8,128)S(1)}, u32[]{:S(2)}, u32[]{:S(2)}) collective-permute-start(f32[16,128]{1,0:T(8,128)S(1)} %slice.36), channel_id=1, source_target_pairs={{0,1},{1,0},{2,3},{3,2},{4,5},{5,4},{6,7},{7,6},{8,9},{9,8},{10,11... | collective-permute-start | bytes 24584 | tf_op jit(solution)/shard_map/ppermute | solution.py:304
  60.0 0.6 copy-start.3
where the time goes:
time: 63.2 us; the launch traced here: 62.9 us
  Pallas kernels  21 us (33%)
  blocking collectives  20.3 us (32%)
  starting transfers between devices  10.6 us (17%)
  waiting for transfers between devices  6.29 us (10%)
  local copies, waits for them, and re-layouts  3.74 us (6%)
  between operations  0.72 us (1%)
    all_to_all x1, blocking collectives, local(): got = lax.all_to_all(sent, 'grid', split_axis=0, concat_axis=0, tiled=True)  20.3 us
    pallas_call x1, Pallas kernels, diffuse(): pl.pallas_call(diffuse_kernel, out_shape=jax.ShapeDtypeStruct((members, 8...  18.7 us
    ppermute x1, starting transfers between devices, local(): other = lax.ppermute(total[:8 * SHARED], 'space', pair)  7.28 us
    ppermute x1, waiting for transfers between devices, local(): lax.ppermute(jnp.concatenate([den[ROWS - LEFT:], kap[ROWS - LEFT:]], axis...  5.46 us
    ppermute x1, starting transfers between devices, local(): lax.ppermute(jnp.concatenate([den[:RIGHT], kap[:RIGHT]], axis=0), 'space'...  3.28 us
    pallas_call x1, Pallas kernels, spread(): pl.pallas_call(spread_kernel, out_shape=jax.ShapeDtypeStruct((ROWS, NY, N...  2.31 us
    unnamed x8, local copies, waits for them, and re-layouts  1.58 us
  transfers between devices with their start and end apart: 3, of which 2 were waited for; matrix products, arithmetic and copies ran while one was open for 2% of the time, Pallas kernels for 0%

commit v1 on v0

--- a/solution.py
+++ b/solution.py
@@ -17,6 +17,8 @@
 LEFT = ITERS
 RIGHT = ITERS + 1
 TALL = LEFT + ROWS + RIGHT
+LOAD_UNROLL = 4
+ROOM = 24 * 1024 * 1024
 NY = 64
 NZ = 128
 TOP = 1 << (LOW + SPAN)
@@ -120,68 +122,126 @@
 
 
 def fetch(ref, index):
-    return jnp.stack([ref[index, pl.ds(v, 8, 8), :] for v in range(8)], axis=0)
-
-
-def advance(f_ref, cx_ref, cy_ref, cz_ref, start, count):
-    def one(i, here, flux):
-        after = f_ref[i + 1]
-        flux_x = cx_ref[i] * (after - here)
-        flux_y = cy_ref[i] * (next_y(here) - here)
-        flux_z = cz_ref[i] * (next_z(here) - here)
-        f_ref[i] = (here + (flux_x - flux)) + ((flux_y - prev_y(flux_y)) + (flux_z - prev_z(flux_z)))
-        return after, flux_x
-
-    before = f_ref[start - 1]
-    here = f_ref[start]
-    flux = cx_ref[start - 1] * (here - before)
-    unroll = 4
-
-    def body(t, carry):
-        here, flux = carry
-        for k in range(unroll):
-            here, flux = one(start + t * unroll + k, here, flux)
-        return here, flux
-
-    whole = count // unroll
-    if whole:
-        here, flux = lax.fori_loop(0, whole, body, (here, flux))
-    for k in range(whole * unroll, count):
-        here, flux = one(start + k, here, flux)
-
-
-def diffuse_kernel(lev, coef, odd, den, kap, left, right, hy3, hz, out, f_ref, cx_ref, cy_ref, cz_ref):
-    def load_rows(f_src, f_base, k_src, k_base, count, base, carry):
-        def body(t, before):
-            k = fetch(k_src, k_base + t)
-            f_ref[base + t] = fetch(f_src, f_base + t)
-            cx_ref[jnp.maximum(base + t - 1, 0)] = 0.5 * (before + k)
-            cy_ref[base + t] = 0.5 * (k + next_y(k))
-            cz_ref[base + t] = 0.5 * (k + next_z(k))
-            return k
-        return lax.fori_loop(0, count, body, carry)
-
-    k = jnp.zeros((8, 8, 128), jnp.float32)
-    k = load_rows(left, 0, left, LEFT, LEFT, 0, k)
-    k = load_rows(den, 0, kap, 0, ROWS, LEFT, k)
-    k = load_rows(right, 0, right, RIGHT, RIGHT, LEFT + ROWS, k)
+    row = ref.at[index]
+    return jnp.stack([row[pl.ds(v, 8, 8), :] for v in range(8)], axis=0)
+
+
+def step_rows(rows, take, put, coef, keep=None):
+    before, here = take(rows[0] - 1), take(rows[0])
+    flux = coef(0, rows[0] - 1) * (here - before)
+    for i in rows:
+        after = take(i + 1)
+        flux_x = coef(0, i) * (after - here)
+        flux_y = coef(1, i) * (next_y(here) - here)
+        flux_z = coef(2, i) * (next_z(here) - here)
+        if keep is not None:
+            keep(i, here)
+        put(i, (here + (flux_x - flux)) + ((flux_y - prev_y(flux_y)) + (flux_z - prev_z(flux_z))))
+        here, flux = after, flux_x
+
+
+def inner_rows(step):
+    reach = ITERS - step
+    if 2 * reach + 1 >= GAP:
+        return [range(step, ROWS - step)]
+    spans = [range(n - reach, min(n + reach + 1, ROWS - step)) for n in range(GAP, ROWS, GAP)]
+    return [r for r in spans if len(r)]
+
+
+def inner_kernel(den, kap, hy3, hz, f_ref, c_ref, old_l, old_r, ends, nodal):
+    def load(t, _):
+        k = fetch(kap, t)
+        after = fetch(kap, jnp.minimum(t + 1, ROWS - 1))
+        f_ref[t] = fetch(den, t)
+        c_ref[0, t] = 0.5 * (k + after)
+        c_ref[1, t] = 0.5 * (k + next_y(k))
+        c_ref[2, t] = 0.5 * (k + next_z(k))
+        return 0
+
+    lax.fori_loop(0, ROWS, load, 0, unroll=LOAD_UNROLL)
+    ends[0] = fetch(kap, 0)
+    ends[1] = fetch(kap, ROWS - 1)
+
+    for step in range(1, ITERS + 1):
+        for rows in inner_rows(step):
+            def keep(i, value, step=step):
+                if i == step and step <= 4:
+                    old_l[step - 1] = value
+                if i == ROWS - 1 - step:
+                    old_r[step - 1] = value
+
+            def put(i, value):
+                f_ref[i] = value
+
+            step_rows(rows, lambda i: f_ref[i], put, lambda a, i: c_ref[a, i], keep)
+    old_r[ITERS - 1] = f_ref[ROWS - 1 - ITERS]
+    hierarchize([f_ref[GAP], f_ref[2 * GAP]], hy3, hz, nodal)
+
+
+def hierarchize(rows, hy3, hz, out):
+    planes = [rows_dot(hy3[...], row.reshape(NY, NZ)) for row in rows]
+    out[...] = lanes_dot(jnp.concatenate(planes, axis=0), hz[...]).reshape(out.shape)
+
+
+def edge_kernel(lev, coef, odd, f_in, c_in, old_l, old_r, ends, nodal_in, left, right, hy3, hz, out, f_new, c_new, nodal):
+    fresh = set()
+
+    def take(i):
+        return f_new[i + LEFT] if i in fresh or not 0 <= i < ROWS else f_in[i]
+
+    def put(i, value):
+        fresh.add(i)
+        f_new[i + LEFT] = value
+
+    def coef_at(a, i):
+        return c_in[a, i] if 0 <= i < ROWS - 1 or (a and i == ROWS - 1) else c_new[a, i + LEFT]
+
+    def prepare(source, first, count, edge_row, edge_k):
+        before = None
+        for t in range(count):
+            i = first + t
+            k = fetch(source, count + t)
+            f_new[i + LEFT] = fetch(source, t)
+            c_new[1, i + LEFT] = 0.5 * (k + next_y(k))
+            c_new[2, i + LEFT] = 0.5 * (k + next_z(k))
+            if before is not None:
+                c_new[0, i - 1 + LEFT] = 0.5 * (before + k)
+            if i == edge_row + 1:
+                c_new[0, edge_row + LEFT] = 0.5 * (edge_k + k)
+            if i == edge_row:
+                c_new[0, edge_row + LEFT] = 0.5 * (edge_k + k)
+            before = k
+
+    prepare(left, -LEFT, LEFT, -1, ends[0])
+    prepare(right, ROWS, RIGHT, ROWS - 1, ends[1])
 
     for step in range(1, ITERS + 1):
         reach = ITERS - step
-        if 2 * reach + 1 >= GAP:
-            advance(f_ref, cx_ref, cy_ref, cz_ref, LEFT - reach, ROWS + 2 * reach + 1)
+        if step <= 4:
+            lefts, rights = [range(-reach, step)], [range(ROWS - step, ROWS + reach + 1)]
         else:
-            def node(n, _, reach=reach):
-                advance(f_ref, cx_ref, cy_ref, cz_ref, LEFT + n * GAP - reach, 2 * reach + 1)
-                return 0
-            lax.fori_loop(0, NODES, node, 0)
-
-    planes = []
-    for n in range(NODES):
-        plane = f_ref[LEFT + n * GAP].reshape(NY, NZ)
-        planes.append(rows_dot(hy3[...], plane))
-    nodal = lanes_dot(jnp.concatenate(planes, axis=0), hz[...]).reshape(NODES, 8, 8, 128)
-
+            lefts = [range(-reach, reach + 1)]
+            rights = [range(ROWS - step, ROWS - step + 1), range(ROWS - reach, ROWS + reach + 1)]
+
+        def take_l(i, step=step):
+            return old_l[step - 1] if i == step and step <= 4 else take(i)
+
+        def take_r(i, step=step):
+            return old_r[step - 1] if i == ROWS - 1 - step else take(i)
+
+        for rows in lefts:
+            step_rows(rows, take_l, lambda i, v: put(i, v), coef_at)
+        for k, rows in enumerate(rights):
+            if k:
+                step_rows(rows, take, lambda i, v: put(i, v), coef_at)
+            else:
+                step_rows(rows, take_r, lambda i, v: put(i, v), coef_at)
+
+    hierarchize([take(0), take(3 * GAP), take(4 * GAP)], hy3, hz, nodal)
+    finish(lev, coef, odd, [nodal.at[0], nodal_in.at[0], nodal_in.at[1], nodal.at[1], nodal.at[2]], out)
+
+
+def finish(lev, coef, odd, nodal, out):
     level_x, level_y, level_z = lev[0, 0], lev[0, 1], lev[0, 2]
     weight = coef[0].astype(jnp.float32)
     swapped = odd[0] == 1
@@ -190,7 +250,7 @@
     width_z = lax.shift_left(1, level_z)
 
     def planes_of(group):
-        u = [nodal[n, group] for n in range(NODES)]
+        u = [nodal[n][group] for n in range(NODES)]
         outer = jnp.where(swapped, u[4], u[0])
         inner = jnp.where(swapped, u[0], u[4])
         return (
@@ -260,20 +320,80 @@
 
 VMEM = pl.BlockSpec(memory_space=pltpu.VMEM)
 SMEM = pl.BlockSpec(memory_space=pltpu.SMEM)
+FAR = pl.BlockSpec(memory_space=pltpu.HBM)
+
+
+def send_kernel(den, kap, up, down, sem):
+    copies = [
+        pltpu.make_async_copy(den.at[pl.ds(ROWS - LEFT, LEFT)], up.at[pl.ds(0, LEFT)], sem.at[0]),
+        pltpu.make_async_copy(kap.at[pl.ds(ROWS - LEFT, LEFT)], up.at[pl.ds(LEFT, LEFT)], sem.at[1]),
+        pltpu.make_async_copy(den.at[pl.ds(0, RIGHT)], down.at[pl.ds(0, RIGHT)], sem.at[2]),
+        pltpu.make_async_copy(kap.at[pl.ds(0, RIGHT)], down.at[pl.ds(RIGHT, RIGHT)], sem.at[3]),
+    ]
+    for copy in copies:
+        copy.start()
+    for copy in copies:
+        copy.wait()
+
+
+def params(room=ROOM):
+    return pltpu.CompilerParams(vmem_limit_bytes=room)
+
+
+def rows_shape(*lead):
+    return jax.ShapeDtypeStruct((*lead, 8, 8, 128), jnp.float32)
+
+
+def send(den, kap, interpret=False):
+    return pl.pallas_call(
+        send_kernel,
+        out_shape=(
+            jax.ShapeDtypeStruct((2 * LEFT, NY, NZ), jnp.float32),
+            jax.ShapeDtypeStruct((2 * RIGHT, NY, NZ), jnp.float32),
+        ),
+        in_specs=[FAR] * 2,
+        out_specs=(VMEM, VMEM),
+        scratch_shapes=[pltpu.SemaphoreType.DMA((4,))],
+        compiler_params=params(8 * 1024 * 1024),
+        interpret=interpret,
+        name="send",
+    )(den, kap)
+
+
+def inner(den, kap, interpret=False):
+    hy3, hz, _, _ = constants()
+    return pl.pallas_call(
+        inner_kernel,
+        out_shape=(rows_shape(ROWS), rows_shape(3, ROWS), rows_shape(4), rows_shape(ITERS), rows_shape(2), rows_shape(2)),
+        in_specs=[VMEM] * 4,
+        out_specs=(VMEM,) * 6,
+        compiler_params=params(),
+        cost_estimate=pl.CostEstimate(flops=20_000_000, bytes_accessed=8_000_000, transcendentals=0),
+        interpret=interpret,
+        name="inner",
+    )(den, kap, jnp.asarray(hy3, jnp.bfloat16), jnp.asarray(hz, jnp.bfloat16))
+
+
+def edge(members, levels, coefs, odd, state, left, right, interpret=False):
+    hy3, hz, _, _ = constants()
+    return pl.pallas_call(
+        edge_kernel,
+        out_shape=jax.ShapeDtypeStruct((members, 8 * TILES, 128), jnp.float32),
+        in_specs=[SMEM] * 3 + [VMEM] * 10,
+        out_specs=VMEM,
+        scratch_shapes=[
+            pltpu.VMEM((TALL, 8, 8, 128), jnp.float32),
+            pltpu.VMEM((3, TALL, 8, 8, 128), jnp.float32),
+            pltpu.VMEM((3, 8, 8, 128), jnp.float32),
+        ],
+        compiler_params=params(),
+        interpret=interpret,
+        name="edge",
+    )(levels, coefs, odd, *state, left, right, jnp.asarray(hy3, jnp.bfloat16), jnp.asarray(hz, jnp.bfloat16))
 
 
 def diffuse(members, levels, coefs, odd, den, kap, left, right, interpret=False):
-    hy3, hz, _, _ = constants()
-    work = pltpu.VMEM((TALL, 8, 8, 128), jnp.float32)
-    return pl.pallas_call(
-        diffuse_kernel,
-        out_shape=jax.ShapeDtypeStruct((members, 8 * TILES, 128), jnp.float32),
-        in_specs=[SMEM] * 3 + [VMEM] * 6,
-        out_specs=VMEM,
-        scratch_shapes=[work] * 4,
-        interpret=interpret,
-        name="diffuse",
-    )(levels, coefs, odd, den, kap, left, right, jnp.asarray(hy3, jnp.bfloat16), jnp.asarray(hz, jnp.bfloat16))
+    return edge(members, levels, coefs, odd, inner(den, kap, interpret), left, right, interpret)
 
 
 def spread(levels, odd, mine, other, interpret=False):
@@ -283,6 +403,7 @@
         out_shape=jax.ShapeDtypeStruct((ROWS, NY, NZ), jnp.float32),
         in_specs=[SMEM] * 2 + [VMEM] * 4,
         out_specs=VMEM,
+        compiler_params=params(),
         interpret=interpret,
         name="spread",
     )(levels, odd, mine, other, jnp.asarray(dy3, jnp.bfloat16), jnp.asarray(dz, jnp.bfloat16))
@@ -295,8 +416,9 @@
     up = [(i, (i + 1) % space) for i in range(space)]
     down = [(j, i) for i, j in up]
     pair = [(i, i ^ 1) for i in range(space)]
-    left = lax.ppermute(jnp.concatenate([den[ROWS - LEFT :], kap[ROWS - LEFT :]], axis=0), "space", up)
-    right = lax.ppermute(jnp.concatenate([den[:RIGHT], kap[:RIGHT]], axis=0), "space", down)
+    going_up, going_down = send(den, kap)
+    left = lax.ppermute(going_up, "space", up)
+    right = lax.ppermute(going_down, "space", down)
     odd = (lax.axis_index("space") % 2).astype(jnp.int32)[None]
     sent = diffuse(grid, levels, coefs, odd, den, kap, left, right)
     got = lax.all_to_all(sent, "grid", split_axis=0, concat_axis=0, tiled=True)

time: 63.2 us -> 55.3 us (0.87)
  waiting for transfers between devices: 6.29 us -> 0.83 us
  starting transfers between devices: 10.6 us -> 6.42 us
  local copies, waits for them, and re-layouts: 3.74 us -> 6.44 us
    ppermute x2, waiting for transfers between devices: 5.46 us -> 0.01 us  [the longest x1 0.01 us: local(): left = lax.ppermute(going_up, 'space', up)]
    unnamed x8 -> x18, local copies, waits for them, and re-layouts: 1.58 us -> 6.44 us
    ppermute x1, starting transfers between devices: 7.28 us -> 3.14 us  [local(): other = lax.ppermute(total[:8 * SHARED], 'space', pair)]
    slice x2 -> x0, local copies, waits for them, and re-layouts: 2.15 us -> none  [the longest x1 1.09 us: local(): kap[:RIGHT]]
    pallas_call x1 -> x3, Pallas kernels: 18.7 us -> 18.5 us  [the longest x1 11.2 us: inner(): pl.pallas_call(inner_kernel, out_shape=(rows_shape(ROWS), rows_shape(3, R...]
  transfers between devices with their start and end apart: 3 -> 3, of which waited for: 2 -> 1; matrix products, arithmetic and copies ran while one was open for 2% -> 0% of each run, Pallas kernels for 0% -> 20%
where the time goes in v1:
time: 55.3 us; the launch traced here: 54.9 us
  Pallas kernels  20.5 us (37%)
  blocking collectives  20 us (36%)
  local copies, waits for them, and re-layouts  6.44 us (12%)
  starting transfers between devices  6.42 us (12%)
  waiting for transfers between devices  0.83 us (2%)
  between operations  0.75 us (1%)
    all_to_all x1, blocking collectives, local(): got = lax.all_to_all(sent, 'grid', split_axis=0, concat_axis=0, tiled=True)  20 us
    pallas_call x1, Pallas kernels, inner(): pl.pallas_call(inner_kernel, out_shape=(rows_shape(ROWS), rows_shape(3, R...  11.2 us
    pallas_call x1, Pallas kernels, edge(): pl.pallas_call(edge_kernel, out_shape=jax.ShapeDtypeStruct((members, 8 *...  7.11 us
    unnamed x18, local copies, waits for them, and re-layouts  6.44 us
    ppermute x1, starting transfers between devices, local(): right = lax.ppermute(going_down, 'space', down)  3.28 us
    ppermute x1, starting transfers between devices, local(): other = lax.ppermute(total[:8 * SHARED], 'space', pair)  3.14 us
    pallas_call x1, Pallas kernels, spread(): pl.pallas_call(spread_kernel, out_shape=jax.ShapeDtypeStruct((ROWS, NY, N...  2.03 us
  transfers between devices with their start and end apart: 3, of which 1 were waited for; matrix products, arithmetic and copies ran while one was open for 0% of the time, Pallas kernels for 20%

profile of v1, /device:TPU:1, one launch (start us, length us, event | category | flops | bytes accessed | tf_op | source)
XLA Modules:
  0.0 54.9 jit_solution(17193485859998967580)
XLA Ops:
  0.0 0.0 copy-start.8
  0.0 0.0 copy-start
  0.0 1.2 %copy-done = f32[1,32,64,128]{3,2,1,0:T(8,128)S(1)} copy-done((f32[1,32,64,128]{3,2,1,0:T(8,128)S(1)}, f32[1,32,64,128]{3,2,1,0:T(8,128)}, u32[]{:S(2)}) %copy-start) | copy-done | bytes 1048600
  1.2 0.0 copy-start.2
  1.2 1.2 %copy-done.2 = f32[1,32,64,128]{3,2,1,0:T(8,128)S(1)} copy-done((f32[1,32,64,128]{3,2,1,0:T(8,128)S(1)}, f32[1,32,64,128]{3,2,1,0:T(8,128)}, u32[]{:S(2)}) %copy-start.2) | copy-done | bytes 1048600
  2.5 0.2 send.1
  2.7 3.3 %collective-permute-start.1 = (f32[18,64,128]{2,1,0:T(8,128)S(1)}, f32[18,64,128]{2,1,0:T(8,128)S(1)}, u32[]{:S(2)}, u32[]{:S(2)}) collective-permute-start(f32[18,64,128]{2,1,0:T(8,128)S(1)} %get-tuple-element.20), channel_id=1, source_target_pairs={{1,0},{2,1},{3,2},{4,3},{5,4},{6,5},{7,6},{8,7},{9,8},{10,9},{11,1... | collective-permute-start | bytes 1769480 | tf_op jit(solution)/shard_map/ppermute | solution.py:421
  5.9 0.0 collective-permute-start
  6.6 0.0 copy-start.1
  6.6 1.2 %copy-done.1 = f32[1,32,64,128]{3,2,1,0:T(8,128)S(1)} copy-done((f32[1,32,64,128]{3,2,1,0:T(8,128)S(1)}, f32[1,32,64,128]{3,2,1,0:T(8,128)}, u32[]{:S(2)}) %copy-start.1) | copy-done | bytes 1048600
  7.8 0.0 copy-start.3
  7.8 1.2 %copy-done.3 = f32[1,32,64,128]{3,2,1,0:T(8,128)S(1)} copy-done((f32[1,32,64,128]{3,2,1,0:T(8,128)S(1)}, f32[1,32,64,128]{3,2,1,0:T(8,128)}, u32[]{:S(2)}) %copy-start.3) | copy-done | bytes 1048600
  9.1 0.0 copy-start.4
  9.1 0.8 %copy-done.4 = bf16[128,128]{1,0:T(8,128)(2,1)S(1)} copy-done((bf16[128,128]{1,0:T(8,128)(2,1)S(1)}, bf16[128,128]{1,0:T(8,128)(2,1)}, u32[]{:S(2)}) %copy-start.4) | copy-done | bytes 32792
  9.8 0.0 copy-start.5
  9.8 0.8 %copy-done.5 = bf16[64,192]{1,0:T(8,128)(2,1)S(1)} copy-done((bf16[64,192]{1,0:T(8,128)(2,1)S(1)}, bf16[64,192]{1,0:T(8,128)(2,1)}, u32[]{:S(2)}) %copy-start.5) | copy-done | bytes 24600
  10.6 11.2 %inner.1 = (f32[32,8,8,128]{3,2,1,0:T(8,128)S(1)}, f32[3,32,8,8,128]{4,3,2,1,0:T(8,128)S(1)}, f32[4,8,8,128]{3,2,1,0:T(8,128)S(1)}, f32[8,8,8,128]{3,2,1,0:T(8,1...) custom-call(f32[32,64,128]{2,1,0:T(8,128)S(1)} %bitcast.5, f32[32,64,128]{2,1,0:T(8,128)S(1)} %bitcast.7, ...), custom_call_target="tpu_custom_call" | custom-call | flops 20000000 | bytes 8000000 | tf_op jit(solution)/shard_map/inner/pallas_call | solution.py:365
  21.7 0.0 collective-permute-done.left
  21.7 0.0 collective-permute-done.1.right
  21.8 0.0 copy-done.8
  21.8 0.0 copy-start.6
  21.8 0.0 copy-start.7
  21.8 7.1 %edge.1 = f32[16,24,128]{2,1,0:T(8,128)S(1)} custom-call(s32[1,3]{1,0:T(1,128)S(1)} %copy-done.8, s32[1]{0:T(128)S(6)} %copy.11.coef, s32[1]{0:T(128)} %bitcast.odd, f32[32,8,8,128]{3,2,1,0:T(8,128)S(1)} %get-tuple-element.13.f_in, f32[3,32,8,8,128]{4,3,2,1,0:T(8,128)S(1)} %get-tuple-element.14.c_in, f32[4,8,8,128]{3,2,1,0:T(8,128)S(1)} %get-tuple-element.15.old_l, ...), custom_call_target="tpu_custom_call" | custom-call | tf_op jit(solution)/shard_map/edge/pallas_call | solution.py:379
  28.9 20.0 %all_to_all.5 = f32[16,24,128]{2,1,0:T(8,128)S(1)} all-to-all(f32[16,24,128]{2,1,0:T(8,128)S(1)} %edge.1), channel_id=1, replica_groups=mesh['grid'=16,'space'=16] {'grid'}, dimensions={0} | all-to-all | bytes 393216 | tf_op jit(solution)/shard_map/all_to_all | solution.py:424
  48.9 3.1 %collective-permute-start.2 = (f32[16,128]{1,0:T(8,128)S(1)}, f32[16,128]{1,0:T(8,128)S(1)}, u32[]{:S(2)}, u32[]{:S(2)}) collective-permute-start(f32[16,128]{1,0:T(8,128)S(1)} %slice.4), channel_id=1, source_target_pairs={{0,1},{1,0},{2,3},{3,2},{4,5},{5,4},{6,7},{7,6},{8,9},{9,8},{10,11... | collective-permute-start | bytes 24584 | tf_op jit(solution)/shard_map/ppermute | solution.py:426
  52.1 0.8 %collective-permute-done.2.other = f32[16,128]{1,0:T(8,128)S(1)} collective-permute-done((f32[16,128]{1,0:T(8,128)S(1)}, f32[16,128]{1,0:T(8,128)S(1)}, u32[]{:S(2)}, u32[]{:S(2)}) %collective-permute-start.2) | collective-permute-done | bytes 8224 | tf_op jit(solution)/shard_map/ppermute | solution.py:426
  52.9 0.0 copy-done.6
  52.9 0.0 copy-done.7
  52.9 2.0 %spread.1 = f32[32,64,128]{2,1,0:T(8,128)} custom-call(s32[1,3]{1,0:T(1,128)S(1)} %copy-done.8, s32[1]{0:T(128)} %bitcast.odd, f32[24,128]{1,0:T(8,128)S(1)} %reduce_sum.9.mine, f32[16,128]{1,0:T(8,128)S(1)} %collective-permute-done.2.other, bf16[64,192]{1,0:T(8,128)(2,1)S(1)} %copy-done.7, bf16[128,128]{1,0:T(8,128)(2,1)S(1)} %copy-done.6), custom_call_target="tpu_custom_call" | custom-call | tf_op jit(solution)/shard_map/spread/pallas_call | solution.py:401
  (2 shorter events, 0.0 us)
Async XLA Ops:
  0.0 21.8 %copy-start.8 = (s32[1,3]{1,0:T(1,128)S(1)}, s32[1,3]{1,0:T(1,128)}, u32[]{:S(2)}) copy-start(s32[1,3]{1,0:T(1,128)} %lev.3) | copy-start | bytes 40
  0.0 1.2 %copy-start = (f32[1,32,64,128]{3,2,1,0:T(8,128)S(1)}, f32[1,32,64,128]{3,2,1,0:T(8,128)}, u32[]{:S(2)}) copy-start(f32[1,32,64,128]{3,2,1,0:T(8,128)} %param.10) | copy-start | bytes 3145732
  1.2 1.2 %copy-start.2 = (f32[1,32,64,128]{3,2,1,0:T(8,128)S(1)}, f32[1,32,64,128]{3,2,1,0:T(8,128)}, u32[]{:S(2)}) copy-start(f32[1,32,64,128]{3,2,1,0:T(8,128)} %param.11) | copy-start | bytes 3145732
  2.7 19.1 %collective-permute-start.1 = (f32[18,64,128]{2,1,0:T(8,128)S(1)}, f32[18,64,128]{2,1,0:T(8,128)S(1)}, u32[]{:S(2)}, u32[]{:S(2)}) collective-permute-start(f32[18,64,128]{2,1,0:T(8,128)S(1)} %get-tuple-element.20), channel_id=1, source_target_pairs={{1,0},{2,1},{3,2},{4,3},{5,4},{6,5},{7,6},{8,7},{9,8},{10,9},{11,1... | collective-permute-start | bytes 1769480 | tf_op jit(solution)/shard_map/ppermute | solution.py:421
  5.9 15.8 %collective-permute-start = (f32[16,64,128]{2,1,0:T(8,128)S(1)}, f32[16,64,128]{2,1,0:T(8,128)S(1)}, u32[]{:S(2)}, u32[]{:S(2)}) collective-permute-start(f32[16,64,128]{2,1,0:T(8,128)S(1)} %get-tuple-element.19), channel_id=1, source_target_pairs={{0,1},{1,2},{2,3},{3,4},{4,5},{5,6},{6,7},{7,8},{8,9},{9,10},{10,1... | collective-permute-start | bytes 1572872 | tf_op jit(solution)/shard_map/ppermute | solution.py:420
  6.6 1.2 %copy-start.1 = (f32[1,32,64,128]{3,2,1,0:T(8,128)S(1)}, f32[1,32,64,128]{3,2,1,0:T(8,128)}, u32[]{:S(2)}) copy-start(f32[1,32,64,128]{3,2,1,0:T(8,128)} %param.10) | copy-start | bytes 3145732
  7.8 1.2 %copy-start.3 = (f32[1,32,64,128]{3,2,1,0:T(8,128)S(1)}, f32[1,32,64,128]{3,2,1,0:T(8,128)}, u32[]{:S(2)}) copy-start(f32[1,32,64,128]{3,2,1,0:T(8,128)} %param.11) | copy-start | bytes 3145732
  9.1 0.8 %copy-start.4 = (bf16[128,128]{1,0:T(8,128)(2,1)S(1)}, bf16[128,128]{1,0:T(8,128)(2,1)}, u32[]{:S(2)}) copy-start(bf16[128,128]{1,0:T(8,128)(2,1)} %constant.28.clone.hz) | copy-start | bytes 98308
  9.8 0.8 %copy-start.5 = (bf16[64,192]{1,0:T(8,128)(2,1)S(1)}, bf16[64,192]{1,0:T(8,128)(2,1)}, u32[]{:S(2)}) copy-start(bf16[64,192]{1,0:T(8,128)(2,1)} %constant.27.clone.hy3) | copy-start | bytes 73732
  21.8 31.1 %copy-start.6 = (bf16[128,128]{1,0:T(8,128)(2,1)S(1)}, bf16[128,128]{1,0:T(8,128)(2,1)}, u32[]{:S(2)}) copy-start(bf16[128,128]{1,0:T(8,128)(2,1)} %constant.30.clone.dz) | copy-start | bytes 98308
  21.8 31.1 %copy-start.7 = (bf16[64,192]{1,0:T(8,128)(2,1)S(1)}, bf16[64,192]{1,0:T(8,128)(2,1)}, u32[]{:S(2)}) copy-start(bf16[64,192]{1,0:T(8,128)(2,1)} %constant.29.clone.dy3) | copy-start | bytes 73732
  48.9 4.0 %collective-permute-start.2 = (f32[16,128]{1,0:T(8,128)S(1)}, f32[16,128]{1,0:T(8,128)S(1)}, u32[]{:S(2)}, u32[]{:S(2)}) collective-permute-start(f32[16,128]{1,0:T(8,128)S(1)} %slice.4), channel_id=1, source_target_pairs={{0,1},{1,0},{2,3},{3,2},{4,5},{5,4},{6,7},{7,6},{8,9},{9,8},{10,11... | collective-permute-start | bytes 24584 | tf_op jit(solution)/shard_map/ppermute | solution.py:426

commit v2 on v1

--- a/solution.py
+++ b/solution.py
@@ -18,6 +18,7 @@
 RIGHT = ITERS + 1
 TALL = LEFT + ROWS + RIGHT
 LOAD_UNROLL = 4
+CHUNK = 8
 ROOM = 24 * 1024 * 1024
 NY = 64
 NZ = 128
@@ -105,14 +106,6 @@
     return total
 
 
-def next_y(row):
-    return jnp.concatenate([row[1:], pltpu.roll(row[0:1], 7, 1)], axis=0)
-
-
-def prev_y(row):
-    return jnp.concatenate([pltpu.roll(row[7:8], 1, 1), row[:7]], axis=0)
-
-
 def next_z(row):
     return pltpu.roll(row, NZ - 1, 2)
 
@@ -126,17 +119,27 @@
     return jnp.stack([row[pl.ds(v, 8, 8), :] for v in range(8)], axis=0)
 
 
-def step_rows(rows, take, put, coef, keep=None):
+def row_coefs(k):
+    ahead = jnp.concatenate([k[1:], pltpu.roll(k[0:1], 7, 1)], axis=0)
+    behind = pltpu.roll(k[7:8], 1, 1)
+    cz, czm = 0.5 * (k + next_z(k)), 0.5 * (k + prev_z(k))
+    return 0.5 * (k + ahead), cz, czm, (1.0 - cz) - czm, 0.5 * (k[0] + behind[0])
+
+
+def step_rows(rows, take, put, coef, first_y, keep=None):
     before, here = take(rows[0] - 1), take(rows[0])
     flux = coef(0, rows[0] - 1) * (here - before)
     for i in rows:
         after = take(i + 1)
+        ahead, behind = pltpu.roll(here[0:1], 7, 1), pltpu.roll(here[7:8], 1, 1)
+        flux_y = coef(1, i) * (jnp.concatenate([here[1:], ahead], axis=0) - here)
+        flux_b = first_y(i) * (here[0] - behind[0])
+        along_z = (coef(2, i) * next_z(here) + coef(3, i) * prev_z(here)) + coef(4, i) * here
         flux_x = coef(0, i) * (after - here)
-        flux_y = coef(1, i) * (next_y(here) - here)
-        flux_z = coef(2, i) * (next_z(here) - here)
         if keep is not None:
             keep(i, here)
-        put(i, (here + (flux_x - flux)) + ((flux_y - prev_y(flux_y)) + (flux_z - prev_z(flux_z))))
+        along_y = flux_y - jnp.concatenate([flux_b[None], flux_y[:7]], axis=0)
+        put(i, along_z + ((flux_x - flux) + along_y))
         here, flux = after, flux_x
 
 
@@ -148,19 +151,37 @@
     return [r for r in spans if len(r)]
 
 
-def inner_kernel(den, kap, hy3, hz, f_ref, c_ref, old_l, old_r, ends, nodal):
-    def load(t, _):
-        k = fetch(kap, t)
-        after = fetch(kap, jnp.minimum(t + 1, ROWS - 1))
-        f_ref[t] = fetch(den, t)
-        c_ref[0, t] = 0.5 * (k + after)
-        c_ref[1, t] = 0.5 * (k + next_y(k))
-        c_ref[2, t] = 0.5 * (k + next_z(k))
-        return 0
-
-    lax.fori_loop(0, ROWS, load, 0, unroll=LOAD_UNROLL)
-    ends[0] = fetch(kap, 0)
-    ends[1] = fetch(kap, ROWS - 1)
+def inner_kernel(den, kap, f_ref, c_ref, cl_ref, old_l, old_r, ends, den_v, kap_v, sem):
+    parts = ROWS // CHUNK
+
+    def copies(part):
+        at = pl.ds(part * CHUNK, CHUNK)
+        return (
+            pltpu.make_async_copy(kap.at[at], kap_v.at[at], sem.at[0, part]),
+            pltpu.make_async_copy(den.at[at], den_v.at[at], sem.at[1, part]),
+        )
+
+    for part in range(parts):
+        for copy in copies(part):
+            copy.start()
+    before = jnp.zeros((8, 8, 128), jnp.float32)
+    for part in range(parts):
+        for copy in copies(part):
+            copy.wait()
+
+        def load(t, before):
+            for u in range(LOAD_UNROLL):
+                i = part * CHUNK + t * LOAD_UNROLL + u
+                k = fetch(kap_v, i)
+                f_ref[i] = fetch(den_v, i)
+                c_ref[0, jnp.maximum(i - 1, 0)] = 0.5 * (before + k)
+                c_ref[1, i], c_ref[2, i], c_ref[3, i], c_ref[4, i], cl_ref[i] = row_coefs(k)
+                before = k
+            return before
+
+        before = lax.fori_loop(0, CHUNK // LOAD_UNROLL, load, before)
+    ends[0] = fetch(kap_v, 0)
+    ends[1] = before
 
     for step in range(1, ITERS + 1):
         for rows in inner_rows(step):
@@ -173,9 +194,8 @@
             def put(i, value):
                 f_ref[i] = value
 
-            step_rows(rows, lambda i: f_ref[i], put, lambda a, i: c_ref[a, i], keep)
+            step_rows(rows, lambda i: f_ref[i], put, lambda a, i: c_ref[a, i], lambda i: cl_ref[i], keep)
     old_r[ITERS - 1] = f_ref[ROWS - 1 - ITERS]
-    hierarchize([f_ref[GAP], f_ref[2 * GAP]], hy3, hz, nodal)
 
 
 def hierarchize(rows, hy3, hz, out):
@@ -183,7 +203,7 @@
     out[...] = lanes_dot(jnp.concatenate(planes, axis=0), hz[...]).reshape(out.shape)
 
 
-def edge_kernel(lev, coef, odd, f_in, c_in, old_l, old_r, ends, nodal_in, left, right, hy3, hz, out, f_new, c_new, nodal):
+def edge_kernel(lev, coef, odd, f_in, c_in, cl_in, old_l, old_r, ends, left, right, hy3, hz, out, f_new, c_new, cl_new, nodal):
     fresh = set()
 
     def take(i):
@@ -195,6 +215,9 @@
 
     def coef_at(a, i):
         return c_in[a, i] if 0 <= i < ROWS - 1 or (a and i == ROWS - 1) else c_new[a, i + LEFT]
+
+    def first_y(i):
+        return cl_in[i] if 0 <= i < ROWS else cl_new[i + LEFT]
 
     def prepare(source, first, count, edge_row, edge_k):
         before = None
@@ -202,8 +225,8 @@
             i = first + t
             k = fetch(source, count + t)
             f_new[i + LEFT] = fetch(source, t)
-            c_new[1, i + LEFT] = 0.5 * (k + next_y(k))
-            c_new[2, i + LEFT] = 0.5 * (k + next_z(k))
+            at = i + LEFT
+            c_new[1, at], c_new[2, at], c_new[3, at], c_new[4, at], cl_new[at] = row_coefs(k)
             if before is not None:
                 c_new[0, i - 1 + LEFT] = 0.5 * (before + k)
             if i == edge_row + 1:
@@ -229,16 +252,14 @@
         def take_r(i, step=step):
             return old_r[step - 1] if i == ROWS - 1 - step else take(i)
 
-        for rows in lefts:
-            step_rows(rows, take_l, lambda i, v: put(i, v), coef_at)
-        for k, rows in enumerate(rights):
-            if k:
-                step_rows(rows, take, lambda i, v: put(i, v), coef_at)
-            else:
-                step_rows(rows, take_r, lambda i, v: put(i, v), coef_at)
-
-    hierarchize([take(0), take(3 * GAP), take(4 * GAP)], hy3, hz, nodal)
-    finish(lev, coef, odd, [nodal.at[0], nodal_in.at[0], nodal_in.at[1], nodal.at[1], nodal.at[2]], out)
+        for k in range(max(len(lefts), len(rights))):
+            if k < len(lefts):
+                step_rows(lefts[k], take_l, put, coef_at, first_y)
+            if k < len(rights):
+                step_rows(rights[k], take if k else take_r, put, coef_at, first_y)
+
+    hierarchize([take(n * GAP) for n in range(NODES)], hy3, hz, nodal)
+    finish(lev, coef, odd, nodal, out)
 
 
 def finish(lev, coef, odd, nodal, out):
@@ -250,7 +271,7 @@
     width_z = lax.shift_left(1, level_z)
 
     def planes_of(group):
-        u = [nodal[n][group] for n in range(NODES)]
+        u = [nodal[n, group] for n in range(NODES)]
         outer = jnp.where(swapped, u[4], u[0])
         inner = jnp.where(swapped, u[0], u[4])
         return (
@@ -344,6 +365,10 @@
     return jax.ShapeDtypeStruct((*lead, 8, 8, 128), jnp.float32)
 
 
+def far(x):
+    return pltpu.with_memory_space_constraint(x, pltpu.HBM)
+
+
 def send(den, kap, interpret=False):
     return pl.pallas_call(
         send_kernel,
@@ -357,21 +382,29 @@
         compiler_params=params(8 * 1024 * 1024),
         interpret=interpret,
         name="send",
-    )(den, kap)
+    )(far(den), far(kap))
 
 
 def inner(den, kap, interpret=False):
-    hy3, hz, _, _ = constants()
+    rows = rows_shape(ROWS)
     return pl.pallas_call(
         inner_kernel,
-        out_shape=(rows_shape(ROWS), rows_shape(3, ROWS), rows_shape(4), rows_shape(ITERS), rows_shape(2), rows_shape(2)),
-        in_specs=[VMEM] * 4,
+        out_shape=(
+            rows,
+            rows_shape(5, ROWS),
+            jax.ShapeDtypeStruct((ROWS, 8, 128), jnp.float32),
+            rows_shape(4),
+            rows_shape(ITERS),
+            rows_shape(2),
+        ),
+        in_specs=[FAR] * 2,
         out_specs=(VMEM,) * 6,
+        scratch_shapes=[pltpu.VMEM((ROWS, NY, NZ), jnp.float32)] * 2 + [pltpu.SemaphoreType.DMA((2, ROWS // CHUNK))],
         compiler_params=params(),
         cost_estimate=pl.CostEstimate(flops=20_000_000, bytes_accessed=8_000_000, transcendentals=0),
         interpret=interpret,
         name="inner",
-    )(den, kap, jnp.asarray(hy3, jnp.bfloat16), jnp.asarray(hz, jnp.bfloat16))
+    )(far(den), far(kap))
 
 
 def edge(members, levels, coefs, odd, state, left, right, interpret=False):
@@ -383,8 +416,9 @@
         out_specs=VMEM,
         scratch_shapes=[
             pltpu.VMEM((TALL, 8, 8, 128), jnp.float32),
-            pltpu.VMEM((3, TALL, 8, 8, 128), jnp.float32),
-            pltpu.VMEM((3, 8, 8, 128), jnp.float32),
+            pltpu.VMEM((5, TALL, 8, 8, 128), jnp.float32),
+            pltpu.VMEM((TALL, 8, 128), jnp.float32),
+            pltpu.VMEM((NODES, 8, 8, 128), jnp.float32),
         ],
         compiler_params=params(),
         interpret=interpret,

time: 55.3 us -> 47.1 us (0.85)
  Pallas kernels: 20.5 us -> 11.9 us
  local copies, waits for them, and re-layouts: 6.44 us -> 2.19 us
  starting transfers between devices: 6.42 us -> 9.2 us
  waiting for transfers between devices: 0.83 us -> 2.33 us
    pallas_call x1, Pallas kernels: 11.2 us -> 5.05 us  [inner(): pl.pallas_call(inner_kernel, out_shape=(rows, rows_shape(5, ROWS), jax.Sh...]
    unnamed x18 -> x12, local copies, waits for them, and re-layouts: 6.44 us -> 2.19 us
    pallas_call x1, Pallas kernels: 7.11 us -> 3.61 us  [edge(): pl.pallas_call(edge_kernel, out_shape=jax.ShapeDtypeStruct((members, 8 *...]
    ppermute x1, starting transfers between devices: 3.14 us -> 5.92 us  [local(): other = lax.ppermute(total[:8 * SHARED], 'space', pair)]
    ppermute x1, waiting for transfers between devices: 0.01 us -> 1.12 us  [local(): right = lax.ppermute(going_down, 'space', down)]
    pallas_call x1, Pallas kernels: 0.19 us -> 1.24 us  [send(): pl.pallas_call(send_kernel, out_shape=(jax.ShapeDtypeStruct((2 * LEFT, NY...]
  transfers between devices with their start and end apart: 3 -> 3, of which waited for: 1 -> 3; matrix products, arithmetic and copies ran while one was open for 0% -> 0% of each run, Pallas kernels for 20% -> 11%
where the time goes in v2:
time: 47.1 us; the launch traced here: 46.8 us
  blocking collectives  20.4 us (43%)
  Pallas kernels  11.9 us (25%)
  starting transfers between devices  9.2 us (20%)
  waiting for transfers between devices  2.33 us (5%)
  local copies, waits for them, and re-layouts  2.19 us (5%)
  between operations  0.72 us (2%)
    all_to_all x1, blocking collectives, local(): got = lax.all_to_all(sent, 'grid', split_axis=0, concat_axis=0, tiled=True)  20.4 us
    ppermute x1, starting transfers between devices, local(): other = lax.ppermute(total[:8 * SHARED], 'space', pair)  5.92 us
    pallas_call x1, Pallas kernels, inner(): pl.pallas_call(inner_kernel, out_shape=(rows, rows_shape(5, ROWS), jax.Sh...  5.05 us
    pallas_call x1, Pallas kernels, edge(): pl.pallas_call(edge_kernel, out_shape=jax.ShapeDtypeStruct((members, 8 *...  3.61 us
    ppermute x1, starting transfers between devices, local(): right = lax.ppermute(going_down, 'space', down)  3.28 us
    unnamed x12, local copies, waits for them, and re-layouts  2.19 us
    pallas_call x1, Pallas kernels, spread(): pl.pallas_call(spread_kernel, out_shape=jax.ShapeDtypeStruct((ROWS, NY, N...  2.04 us
    pallas_call x1, Pallas kernels, send(): pl.pallas_call(send_kernel, out_shape=(jax.ShapeDtypeStruct((2 * LEFT, NY...  1.24 us
  transfers between devices with their start and end apart: 3, of which 3 were waited for; matrix products, arithmetic and copies ran while one was open for 0% of the time, Pallas kernels for 11%

profile of v2, /device:TPU:1, one launch (start us, length us, event | category | flops | bytes accessed | tf_op | source)
XLA Modules:
  0.0 46.8 jit_solution(2694434025331804499)
XLA Ops:
  0.0 1.2 %send.1 = (f32[16,64,128]{2,1,0:T(8,128)S(1)}, f32[18,64,128]{2,1,0:T(8,128)S(1)}) custom-call(f32[32,64,128]{2,1,0:T(8,128)} %bitcast.4, f32[32,64,128]{2,1,0:T(8,128)} %bitcast.6), custom_call_target="tpu_custom_call" | custom-call | tf_op jit(solution)/shard_map/send/pallas_call | solution.py:373
  1.2 3.3 %collective-permute-start.1 = (f32[18,64,128]{2,1,0:T(8,128)S(1)}, f32[18,64,128]{2,1,0:T(8,128)S(1)}, u32[]{:S(2)}, u32[]{:S(2)}) collective-permute-start(f32[18,64,128]{2,1,0:T(8,128)S(1)} %get-tuple-element.20), channel_id=1, source_target_pairs={{1,0},{2,1},{3,2},{4,3},{5,4},{6,5},{7,6},{8,7},{9,8},{10,9},{11,1... | collective-permute-start | bytes 1769480 | tf_op jit(solution)/shard_map/ppermute | solution.py:455
  4.5 0.0 collective-permute-start
  5.2 0.0 copy-start.2
  5.2 0.0 copy-start.3
  5.2 0.0 copy-start.5
  5.2 5.0 %inner.1 = (f32[32,8,8,128]{3,2,1,0:T(8,128)S(1)}, f32[5,32,8,8,128]{4,3,2,1,0:T(8,128)S(1)}, f32[32,8,128]{2,1,0:T(8,128)S(1)}, f32[4,8,8,128]{3,2,1,0:T(8,128)...) custom-call(f32[32,64,128]{2,1,0:T(8,128)} %bitcast.5, f32[32,64,128]{2,1,0:T(8,128)} %bitcast.7), custom_call_target="tpu_custom_call" | custom-call | flops 20000000 | bytes 8000000 | tf_op jit(solution)/shard_map/inner/pallas_call | solution.py:390
  10.3 0.4 collective-permute-done.left
  10.7 1.1 %collective-permute-done.1.right = f32[18,64,128]{2,1,0:T(8,128)S(1)} collective-permute-done((f32[18,64,128]{2,1,0:T(8,128)S(1)}, f32[18,64,128]{2,1,0:T(8,128)S(1)}, u32[]{:S(2)}, u32[]{:S(2)}) %collective-permute-start.1) | collective-permute-done | bytes 589856 | tf_op jit(solution)/shard_map/ppermute | solution.py:455
  11.8 0.0 copy-start
  11.8 0.8 %copy-done = bf16[128,128]{1,0:T(8,128)(2,1)S(1)} copy-done((bf16[128,128]{1,0:T(8,128)(2,1)S(1)}, bf16[128,128]{1,0:T(8,128)(2,1)}, u32[]{:S(2)}) %copy-start) | copy-done | bytes 32792
  12.5 0.0 copy-start.1
  12.5 0.8 %copy-done.1 = bf16[64,192]{1,0:T(8,128)(2,1)S(1)} copy-done((bf16[64,192]{1,0:T(8,128)(2,1)S(1)}, bf16[64,192]{1,0:T(8,128)(2,1)}, u32[]{:S(2)}) %copy-start.1) | copy-done | bytes 24600
  13.3 0.0 copy-start.4
  13.3 0.7 %copy-done.4 = s32[1,3]{1,0:T(1,128)S(1)} copy-done((s32[1,3]{1,0:T(1,128)S(1)}, s32[1,3]{1,0:T(1,128)}, u32[]{:S(2)}) %copy-start.4) | copy-done | bytes 36
  14.0 3.6 %edge.1 = f32[16,24,128]{2,1,0:T(8,128)S(1)} custom-call(s32[1,3]{1,0:T(1,128)S(1)} %copy-done.4, s32[1]{0:T(128)S(6)} %copy.9.coef, s32[1]{0:T(128)} %bitcast.odd, f32[32,8,8,128]{3,2,1,0:T(8,128)S(1)} %get-tuple-element.13.f_in, f32[5,32,8,8,128]{4,3,2,1,0:T(8,128)S(1)} %get-tuple-element.14.c_in, f32[32,8,128]{2,1,0:T(8,128)S(1)} %get-tuple-element.15.cl_in, ...), custom_call_target="tpu_custom_call" | custom-call | tf_op jit(solution)/shard_map/edge/pallas_call | solution.py:412
  17.6 20.4 %all_to_all.5 = f32[16,24,128]{2,1,0:T(8,128)S(1)} all-to-all(f32[16,24,128]{2,1,0:T(8,128)S(1)} %edge.1), channel_id=1, replica_groups=mesh['grid'=16,'space'=16] {'grid'}, dimensions={0} | all-to-all | bytes 393216 | tf_op jit(solution)/shard_map/all_to_all | solution.py:458
  38.0 5.9 %collective-permute-start.2 = (f32[16,128]{1,0:T(8,128)S(1)}, f32[16,128]{1,0:T(8,128)S(1)}, u32[]{:S(2)}, u32[]{:S(2)}) collective-permute-start(f32[16,128]{1,0:T(8,128)S(1)} %slice.4), channel_id=1, source_target_pairs={{0,1},{1,0},{2,3},{3,2},{4,5},{5,4},{6,7},{7,6},{8,9},{9,8},{10,11... | collective-permute-start | bytes 24584 | tf_op jit(solution)/shard_map/ppermute | solution.py:460
  43.9 0.8 %collective-permute-done.2.other = f32[16,128]{1,0:T(8,128)S(1)} collective-permute-done((f32[16,128]{1,0:T(8,128)S(1)}, f32[16,128]{1,0:T(8,128)S(1)}, u32[]{:S(2)}, u32[]{:S(2)}) %collective-permute-start.2) | collective-permute-done | bytes 8224 | tf_op jit(solution)/shard_map/ppermute | solution.py:460
  44.7 0.0 copy-done.2
  44.7 0.0 copy-done.3
  44.8 0.0 copy-done.5
  44.8 2.0 %spread.1 = f32[32,64,128]{2,1,0:T(8,128)} custom-call(s32[1,3]{1,0:T(1,128)S(1)} %copy-done.5, s32[1]{0:T(128)} %bitcast.odd, f32[24,128]{1,0:T(8,128)S(1)} %reduce_sum.9.mine, f32[16,128]{1,0:T(8,128)S(1)} %collective-permute-done.2.other, bf16[64,192]{1,0:T(8,128)(2,1)S(1)} %copy-done.3, bf16[128,128]{1,0:T(8,128)(2,1)S(1)} %copy-done.2), custom_call_target="tpu_custom_call" | custom-call | tf_op jit(solution)/shard_map/spread/pallas_call | solution.py:435
  (2 shorter events, 0.0 us)
Async XLA Ops:
  1.2 10.5 %collective-permute-start.1 = (f32[18,64,128]{2,1,0:T(8,128)S(1)}, f32[18,64,128]{2,1,0:T(8,128)S(1)}, u32[]{:S(2)}, u32[]{:S(2)}) collective-permute-start(f32[18,64,128]{2,1,0:T(8,128)S(1)} %get-tuple-element.20), channel_id=1, source_target_pairs={{1,0},{2,1},{3,2},{4,3},{5,4},{6,5},{7,6},{8,7},{9,8},{10,9},{11,1... | collective-permute-start | bytes 1769480 | tf_op jit(solution)/shard_map/ppermute | solution.py:455
  4.5 6.1 %collective-permute-start = (f32[16,64,128]{2,1,0:T(8,128)S(1)}, f32[16,64,128]{2,1,0:T(8,128)S(1)}, u32[]{:S(2)}, u32[]{:S(2)}) collective-permute-start(f32[16,64,128]{2,1,0:T(8,128)S(1)} %get-tuple-element.19), channel_id=1, source_target_pairs={{0,1},{1,2},{2,3},{3,4},{4,5},{5,6},{6,7},{7,8},{8,9},{9,10},{10,1... | collective-permute-start | bytes 1572872 | tf_op jit(solution)/shard_map/ppermute | solution.py:454
  5.2 39.6 %copy-start.2 = (bf16[128,128]{1,0:T(8,128)(2,1)S(1)}, bf16[128,128]{1,0:T(8,128)(2,1)}, u32[]{:S(2)}) copy-start(bf16[128,128]{1,0:T(8,128)(2,1)} %constant.30.clone.dz) | copy-start | bytes 98308
  5.2 39.5 %copy-start.3 = (bf16[64,192]{1,0:T(8,128)(2,1)S(1)}, bf16[64,192]{1,0:T(8,128)(2,1)}, u32[]{:S(2)}) copy-start(bf16[64,192]{1,0:T(8,128)(2,1)} %constant.29.clone.dy3) | copy-start | bytes 73732
  5.2 39.5 %copy-start.5 = (s32[1,3]{1,0:T(1,128)S(1)}, s32[1,3]{1,0:T(1,128)}, u32[]{:S(2)}) copy-start(s32[1,3]{1,0:T(1,128)} %lev.3) | copy-start | bytes 40
  11.8 0.8 %copy-start = (bf16[128,128]{1,0:T(8,128)(2,1)S(1)}, bf16[128,128]{1,0:T(8,128)(2,1)}, u32[]{:S(2)}) copy-start(bf16[128,128]{1,0:T(8,128)(2,1)} %constant.28.clone.hz) | copy-start | bytes 98308
  12.5 0.8 %copy-start.1 = (bf16[64,192]{1,0:T(8,128)(2,1)S(1)}, bf16[64,192]{1,0:T(8,128)(2,1)}, u32[]{:S(2)}) copy-start(bf16[64,192]{1,0:T(8,128)(2,1)} %constant.27.clone.hy3) | copy-start | bytes 73732
  13.3 0.7 %copy-start.4 = (s32[1,3]{1,0:T(1,128)S(1)}, s32[1,3]{1,0:T(1,128)}, u32[]{:S(2)}) copy-start(s32[1,3]{1,0:T(1,128)} %lev.3) | copy-start | bytes 40
  38.0 6.7 %collective-permute-start.2 = (f32[16,128]{1,0:T(8,128)S(1)}, f32[16,128]{1,0:T(8,128)S(1)}, u32[]{:S(2)}, u32[]{:S(2)}) collective-permute-start(f32[16,128]{1,0:T(8,128)S(1)} %slice.4), channel_id=1, source_target_pairs={{0,1},{1,0},{2,3},{3,2},{4,5},{5,4},{6,7},{7,6},{8,9},{9,8},{10,11... | collective-permute-start | bytes 24584 | tf_op jit(solution)/shard_map/ppermute | solution.py:460

commit v3 on v2

--- a/solution.py
+++ b/solution.py
@@ -82,6 +82,7 @@
 
 
 BLOCKS, TILES = staircase()
+NEED = (LOW, LOW + 1, LOW + 2, LOW + 3, LOW + 3)
 SHARED = 1 + max(b[3] for b in BLOCKS if b[0] < 2)
 
 
@@ -151,7 +152,21 @@
     return [r for r in spans if len(r)]
 
 
-def inner_kernel(den, kap, f_ref, c_ref, cl_ref, old_l, old_r, ends, den_v, kap_v, sem):
+def write_marks(lev, coef, odd, marks):
+    level_x, level_y, level_z = lev[0, 0], lev[0, 1], lev[0, 2]
+    weight = coef[0].astype(jnp.float32)
+    lane = lax.broadcasted_iota(jnp.int32, (8, 128), 1)
+    groups_y = lax.shift_left(1, level_y - LOW)
+    width_z = lax.shift_left(1, level_z)
+    for b, (plane, group, width, _, _) in enumerate(BLOCKS):
+        keep = (lane < jnp.minimum(width_z, width)) & (group < groups_y) & (level_x >= NEED[plane])
+        kept = jnp.where(keep, 1.0, 0.0)
+        marks[b] = kept
+        marks[len(BLOCKS) + b] = weight * kept
+    marks[2 * len(BLOCKS)] = jnp.full((8, 128), odd[0].astype(jnp.float32))
+
+
+def inner_kernel(lev, coef, odd, den, kap, hy3, hz, f_ref, c_ref, cl_ref, old_l, old_r, ends, marks, hy3_v, hz_v, den_v, kap_v, sem, sem_w):
     parts = ROWS // CHUNK
 
     def copies(part):
@@ -164,6 +179,10 @@
     for part in range(parts):
         for copy in copies(part):
             copy.start()
+    weights = [pltpu.make_async_copy(hy3, hy3_v, sem_w.at[0]), pltpu.make_async_copy(hz, hz_v, sem_w.at[1])]
+    for copy in weights:
+        copy.start()
+    write_marks(lev, coef, odd, marks)
     before = jnp.zeros((8, 8, 128), jnp.float32)
     for part in range(parts):
         for copy in copies(part):
@@ -196,6 +215,8 @@
 
             step_rows(rows, lambda i: f_ref[i], put, lambda a, i: c_ref[a, i], lambda i: cl_ref[i], keep)
     old_r[ITERS - 1] = f_ref[ROWS - 1 - ITERS]
+    for copy in weights:
+        copy.wait()
 
 
 def hierarchize(rows, hy3, hz, out):
@@ -203,7 +224,7 @@
     out[...] = lanes_dot(jnp.concatenate(planes, axis=0), hz[...]).reshape(out.shape)
 
 
-def edge_kernel(lev, coef, odd, f_in, c_in, cl_in, old_l, old_r, ends, left, right, hy3, hz, out, f_new, c_new, cl_new, nodal):
+def edge_kernel(f_in, c_in, cl_in, old_l, old_r, ends, marks, hy3, hz, left, right, out, f_new, c_new, cl_new, nodal):
     fresh = set()
 
     def take(i):
@@ -259,16 +280,11 @@
                 step_rows(rights[k], take if k else take_r, put, coef_at, first_y)
 
     hierarchize([take(n * GAP) for n in range(NODES)], hy3, hz, nodal)
-    finish(lev, coef, odd, nodal, out)
-
-
-def finish(lev, coef, odd, nodal, out):
-    level_x, level_y, level_z = lev[0, 0], lev[0, 1], lev[0, 2]
-    weight = coef[0].astype(jnp.float32)
-    swapped = odd[0] == 1
-    lane = lax.broadcasted_iota(jnp.int32, (8, 128), 1)
-    groups_y = lax.shift_left(1, level_y - LOW)
-    width_z = lax.shift_left(1, level_z)
+    finish(marks, nodal, out)
+
+
+def finish(marks, nodal, out):
+    swapped = marks[2 * len(BLOCKS)] > 0.5
 
     def planes_of(group):
         u = [nodal[n, group] for n in range(NODES)]
@@ -282,38 +298,30 @@
             u[3] - 0.5 * (u[2] + u[4]),
         )
 
-    need = (LOW, LOW + 1, LOW + 2, LOW + 3, LOW + 3)
     cache = {}
     tiles = [jnp.zeros((8, 128), jnp.float32)] * TILES
-    for plane, group, width, tile, first in BLOCKS:
+    for b, (plane, group, width, tile, first) in enumerate(BLOCKS):
         if group not in cache:
             cache[group] = planes_of(group)
-        keep = (lane < jnp.minimum(width_z, width)) & (group < groups_y) & (level_x >= need[plane])
-        value = jnp.where(keep, weight * cache[group][plane], 0.0)
+        value = marks[len(BLOCKS) + b] * cache[group][plane]
         tiles[tile] = tiles[tile] + (pltpu.roll(value, first, 1) if first else value)
     for member in range(out.shape[0]):
         for tile in range(TILES):
             out[member, 8 * tile : 8 * tile + 8] = tiles[tile]
 
 
-def spread_kernel(lev, odd, mine, other, dy3, dz, out):
-    level_x, level_y, level_z = lev[0, 0], lev[0, 1], lev[0, 2]
-    swapped = odd[0] == 1
-    lane = lax.broadcasted_iota(jnp.int32, (8, 128), 1)
-    groups_y = lax.shift_left(1, level_y - LOW)
-    width_z = lax.shift_left(1, level_z)
-    need = (LOW, LOW + 1, LOW + 2, LOW + 3, LOW + 3)
+def spread_kernel(marks, mine, other, dy3, dz, out, held, sem):
+    swapped = marks[2 * len(BLOCKS), 0:1] > 0.5
     own = [mine[8 * t : 8 * t + 8] for t in range(TILES)]
     theirs = [other[8 * t : 8 * t + 8] for t in range(SHARED)]
     zero = jnp.zeros((8, 128), jnp.float32)
     planes = [[zero] * 8 for _ in range(5)]
     outer_other = [zero] * 8
-    for plane, group, width, tile, first in BLOCKS:
-        keep = (lane < jnp.minimum(width_z, width)) & (group < groups_y) & (level_x >= need[plane])
+    for b, (plane, group, width, tile, first) in enumerate(BLOCKS):
 
         def pick(source):
             value = pltpu.roll(source, 128 - first, 1) if first else source
-            return jnp.where(keep, value, 0.0)
+            return marks[b] * value
 
         if plane == 0:
             planes[0][group] = pick(own[tile])
@@ -333,10 +341,16 @@
     for n in (n0, n1, n2, n3, n4):
         wide.append(rows_dot(dy3[...], n))
     full = lanes_dot(jnp.concatenate(wide, axis=0), dz[...]).reshape(NODES, NY, NZ)
+    copies = []
     for q in range(NODES - 1):
         slope = (full[q + 1] - full[q]) * (1.0 / GAP)
         for k in range(GAP):
-            out[q * GAP + k] = full[q] + float(k) * slope
+            held[q * GAP + k] = full[q] + float(k) * slope
+        at = pl.ds(q * GAP, GAP)
+        copies.append(pltpu.make_async_copy(held.at[at], out.at[at], sem.at[q]))
+        copies[-1].start()
+    for copy in copies:
+        copy.wait()
 
 
 VMEM = pl.BlockSpec(memory_space=pltpu.VMEM)
@@ -385,8 +399,9 @@
     )(far(den), far(kap))
 
 
-def inner(den, kap, interpret=False):
+def inner(levels, coefs, odd, den, kap, interpret=False):
     rows = rows_shape(ROWS)
+    hy3, hz, _, _ = constants()
     return pl.pallas_call(
         inner_kernel,
         out_shape=(
@@ -396,23 +411,26 @@
             rows_shape(4),
             rows_shape(ITERS),
             rows_shape(2),
+            jax.ShapeDtypeStruct((2 * len(BLOCKS) + 1, 8, 128), jnp.float32),
+            jax.ShapeDtypeStruct(hy3.shape, jnp.bfloat16),
+            jax.ShapeDtypeStruct(hz.shape, jnp.bfloat16),
         ),
-        in_specs=[FAR] * 2,
-        out_specs=(VMEM,) * 6,
-        scratch_shapes=[pltpu.VMEM((ROWS, NY, NZ), jnp.float32)] * 2 + [pltpu.SemaphoreType.DMA((2, ROWS // CHUNK))],
+        in_specs=[SMEM] * 3 + [FAR] * 4,
+        out_specs=(VMEM,) * 9,
+        scratch_shapes=[pltpu.VMEM((ROWS, NY, NZ), jnp.float32)] * 2
+        + [pltpu.SemaphoreType.DMA((2, ROWS // CHUNK)), pltpu.SemaphoreType.DMA((2,))],
         compiler_params=params(),
         cost_estimate=pl.CostEstimate(flops=20_000_000, bytes_accessed=8_000_000, transcendentals=0),
         interpret=interpret,
         name="inner",
-    )(far(den), far(kap))
-
-
-def edge(members, levels, coefs, odd, state, left, right, interpret=False):
-    hy3, hz, _, _ = constants()
+    )(levels, coefs, odd, far(den), far(kap), far(jnp.asarray(hy3, jnp.bfloat16)), far(jnp.asarray(hz, jnp.bfloat16)))
+
+
+def edge(members, state, left, right, interpret=False):
     return pl.pallas_call(
         edge_kernel,
         out_shape=jax.ShapeDtypeStruct((members, 8 * TILES, 128), jnp.float32),
-        in_specs=[SMEM] * 3 + [VMEM] * 10,
+        in_specs=[VMEM] * 11,
         out_specs=VMEM,
         scratch_shapes=[
             pltpu.VMEM((TALL, 8, 8, 128), jnp.float32),
@@ -423,24 +441,21 @@
         compiler_params=params(),
         interpret=interpret,
         name="edge",
-    )(levels, coefs, odd, *state, left, right, jnp.asarray(hy3, jnp.bfloat16), jnp.asarray(hz, jnp.bfloat16))
-
-
-def diffuse(members, levels, coefs, odd, den, kap, left, right, interpret=False):
-    return edge(members, levels, coefs, odd, inner(den, kap, interpret), left, right, interpret)
-
-
-def spread(levels, odd, mine, other, interpret=False):
+    )(*state, left, right)
+
+
+def spread(marks, mine, other, interpret=False):
     _, _, dy3, dz = constants()
     return pl.pallas_call(
         spread_kernel,
         out_shape=jax.ShapeDtypeStruct((ROWS, NY, NZ), jnp.float32),
-        in_specs=[SMEM] * 2 + [VMEM] * 4,
-        out_specs=VMEM,
+        in_specs=[VMEM] * 5,
+        out_specs=FAR,
+        scratch_shapes=[pltpu.VMEM((ROWS, NY, NZ), jnp.float32), pltpu.SemaphoreType.DMA((NODES - 1,))],
         compiler_params=params(),
         interpret=interpret,
         name="spread",
-    )(levels, odd, mine, other, jnp.asarray(dy3, jnp.bfloat16), jnp.asarray(dz, jnp.bfloat16))
+    )(marks, mine, other, jnp.asarray(dy3, jnp.bfloat16), jnp.asarray(dz, jnp.bfloat16))
 
 
 def local(density, kappa, levels, coefs):
@@ -454,11 +469,12 @@
     left = lax.ppermute(going_up, "space", up)
     right = lax.ppermute(going_down, "space", down)
     odd = (lax.axis_index("space") % 2).astype(jnp.int32)[None]
-    sent = diffuse(grid, levels, coefs, odd, den, kap, left, right)
+    state = inner(levels, coefs, odd, den, kap)
+    sent = edge(grid, state, left, right)
     got = lax.all_to_all(sent, "grid", split_axis=0, concat_axis=0, tiled=True)
     total = jnp.sum(got, axis=0)
     other = lax.ppermute(total[: 8 * SHARED], "space", pair)
-    return spread(levels, odd, total, other)[None]
+    return spread(state[6], total, other)[None]
 
 
 def solution(mesh):

time: 47.1 us -> 44 us (0.934)
  local copies, waits for them, and re-layouts: 2.19 us -> 0.66 us
  waiting for transfers between devices: 2.33 us -> 0.83 us
    unnamed x12 -> x6, local copies, waits for them, and re-layouts: 2.19 us -> 0.66 us
    ppermute x1, waiting for transfers between devices: 1.12 us -> 0.01 us  [local(): right = lax.ppermute(going_down, 'space', down)]
    pallas_call x1, Pallas kernels: 5.05 us -> 6.09 us  [inner(): pl.pallas_call(inner_kernel, out_shape=(rows, rows_shape(5, ROWS), jax.Sh...]
    pallas_call x1, Pallas kernels: 2.04 us -> 1.45 us  [spread(): pl.pallas_call(spread_kernel, out_shape=jax.ShapeDtypeStruct((ROWS, NY, N...]
  transfers between devices with their start and end apart: 3 -> 3, of which waited for: 3 -> 1; matrix products, arithmetic and copies ran while one was open for 0% -> 0% of each run, Pallas kernels for 11% -> 14%
where the time goes in v3:
time: 44 us; the launch traced here: 43.8 us
  blocking collectives  20.2 us (46%)
  Pallas kernels  12.2 us (28%)
  starting transfers between devices  9.2 us (21%)
  waiting for transfers between devices  0.83 us (2%)
  between operations  0.72 us (2%)
  local copies, waits for them, and re-layouts  0.66 us (2%)
    all_to_all x1, blocking collectives, local(): got = lax.all_to_all(sent, 'grid', split_axis=0, concat_axis=0, tiled=True)  20.2 us
    pallas_call x1, Pallas kernels, inner(): pl.pallas_call(inner_kernel, out_shape=(rows, rows_shape(5, ROWS), jax.Sh...  6.09 us
    ppermute x1, starting transfers between devices, local(): other = lax.ppermute(total[:8 * SHARED], 'space', pair)  5.92 us
    pallas_call x1, Pallas kernels, edge(): pl.pallas_call(edge_kernel, out_shape=jax.ShapeDtypeStruct((members, 8 *...  3.39 us
    ppermute x1, starting transfers between devices, local(): right = lax.ppermute(going_down, 'space', down)  3.28 us
    pallas_call x1, Pallas kernels, spread(): pl.pallas_call(spread_kernel, out_shape=jax.ShapeDtypeStruct((ROWS, NY, N...  1.45 us
    pallas_call x1, Pallas kernels, send(): pl.pallas_call(send_kernel, out_shape=(jax.ShapeDtypeStruct((2 * LEFT, NY...  1.24 us
  transfers between devices with their start and end apart: 3, of which 1 were waited for; matrix products, arithmetic and copies ran while one was open for 0% of the time, Pallas kernels for 14%

profile of v3, /device:TPU:1, one launch (start us, length us, event | category | flops | bytes accessed | tf_op | source)
XLA Modules:
  0.0 43.8 jit_solution(2877777886358453635)
XLA Ops:
  0.0 1.2 %send.1 = (f32[16,64,128]{2,1,0:T(8,128)S(1)}, f32[18,64,128]{2,1,0:T(8,128)S(1)}) custom-call(f32[32,64,128]{2,1,0:T(8,128)} %bitcast.4, f32[32,64,128]{2,1,0:T(8,128)} %bitcast.6), custom_call_target="tpu_custom_call" | custom-call | tf_op jit(solution)/shard_map/send/pallas_call | solution.py:387
  1.2 3.3 %collective-permute-start.1 = (f32[18,64,128]{2,1,0:T(8,128)S(1)}, f32[18,64,128]{2,1,0:T(8,128)S(1)}, u32[]{:S(2)}, u32[]{:S(2)}) collective-permute-start(f32[18,64,128]{2,1,0:T(8,128)S(1)} %get-tuple-element.26), channel_id=1, source_target_pairs={{1,0},{2,1},{3,2},{4,3},{5,4},{6,5},{7,6},{8,7},{9,8},{10,9},{11,1... | collective-permute-start | bytes 1769480 | tf_op jit(solution)/shard_map/ppermute | solution.py:470
  4.5 0.0 collective-permute-start
  5.2 0.0 copy-start.2
  5.2 0.6 %copy-done.2 = s32[1,3]{1,0:T(1,128)S(1)} copy-done((s32[1,3]{1,0:T(1,128)S(1)}, s32[1,3]{1,0:T(1,128)}, u32[]{:S(2)}) %copy-start.2) | copy-done | bytes 36
  5.8 0.0 copy-start
  5.8 0.0 copy-start.1
  5.8 6.1 %inner.1 = (f32[32,8,8,128]{3,2,1,0:T(8,128)S(1)}, f32[5,32,8,8,128]{4,3,2,1,0:T(8,128)S(1)}, f32[32,8,128]{2,1,0:T(8,128)S(1)}, f32[4,8,8,128]{3,2,1,0:T(8,128)...) custom-call(s32[1,3]{1,0:T(1,128)S(1)} %copy-done.2, ...), custom_call_target="tpu_custom_call" | custom-call | flops 20000000 | bytes 8000000 | tf_op jit(solution)/shard_map/inner/pallas_call | solution.py:405
  11.9 0.0 collective-permute-done.left
  12.0 0.0 collective-permute-done.1.right
  12.0 3.4 %edge.1 = f32[16,24,128]{2,1,0:T(8,128)S(1)} custom-call(f32[32,8,8,128]{3,2,1,0:T(8,128)S(1)} %get-tuple-element.17.f_in, f32[5,32,8,8,128]{4,3,2,1,0:T(8,128)S(1)} %get-tuple-element.18.c_in, f32[32,8,128]{2,1,0:T(8,128)S(1)} %get-tuple-element.19.cl_in, f32[4,8,8,128]{3,2,1,0:T(8,128)S(1)} %get-tuple-element.20.old_l, ...), custom_call_target="tpu_custom_call" | custom-call | tf_op jit(solution)/shard_map/edge/pallas_call | solution.py:430
  15.4 20.2 %all_to_all.5 = f32[16,24,128]{2,1,0:T(8,128)S(1)} all-to-all(f32[16,24,128]{2,1,0:T(8,128)S(1)} %edge.1), channel_id=1, replica_groups=mesh['grid'=16,'space'=16] {'grid'}, dimensions={0} | all-to-all | bytes 393216 | tf_op jit(solution)/shard_map/all_to_all | solution.py:474
  35.6 5.9 %collective-permute-start.2 = (f32[16,128]{1,0:T(8,128)S(1)}, f32[16,128]{1,0:T(8,128)S(1)}, u32[]{:S(2)}, u32[]{:S(2)}) collective-permute-start(f32[16,128]{1,0:T(8,128)S(1)} %slice.4), channel_id=1, source_target_pairs={{0,1},{1,0},{2,3},{3,2},{4,5},{5,4},{6,7},{7,6},{8,9},{9,8},{10,11... | collective-permute-start | bytes 24584 | tf_op jit(solution)/shard_map/ppermute | solution.py:476
  41.5 0.8 %collective-permute-done.2.other = f32[16,128]{1,0:T(8,128)S(1)} collective-permute-done((f32[16,128]{1,0:T(8,128)S(1)}, f32[16,128]{1,0:T(8,128)S(1)}, u32[]{:S(2)}, u32[]{:S(2)}) %collective-permute-start.2) | collective-permute-done | bytes 8224 | tf_op jit(solution)/shard_map/ppermute | solution.py:476
  42.4 0.0 copy-done
  42.4 0.0 copy-done.1
  42.4 1.4 %spread.1 = f32[32,64,128]{2,1,0:T(8,128)} custom-call(f32[33,8,128]{2,1,0:T(8,128)S(1)} %get-tuple-element.16.marks, f32[24,128]{1,0:T(8,128)S(1)} %reduce_sum.9.mine, f32[16,128]{1,0:T(8,128)S(1)} %collective-permute-done.2.other, bf16[64,192]{1,0:T(8,128)(2,1)S(1)} %copy-done.1, bf16[128,128]{1,0:T(8,128)(2,1)S(1)} %copy-done), custom_call_target="tpu_custom_call" | custom-call | tf_op jit(solution)/shard_map/spread/pallas_call | solution.py:449
  (2 shorter events, 0.0 us)
Async XLA Ops:
  1.2 10.7 %collective-permute-start.1 = (f32[18,64,128]{2,1,0:T(8,128)S(1)}, f32[18,64,128]{2,1,0:T(8,128)S(1)}, u32[]{:S(2)}, u32[]{:S(2)}) collective-permute-start(f32[18,64,128]{2,1,0:T(8,128)S(1)} %get-tuple-element.26), channel_id=1, source_target_pairs={{1,0},{2,1},{3,2},{4,3},{5,4},{6,5},{7,6},{8,7},{9,8},{10,9},{11,1... | collective-permute-start | bytes 1769480 | tf_op jit(solution)/shard_map/ppermute | solution.py:470
  4.5 7.4 %collective-permute-start = (f32[16,64,128]{2,1,0:T(8,128)S(1)}, f32[16,64,128]{2,1,0:T(8,128)S(1)}, u32[]{:S(2)}, u32[]{:S(2)}) collective-permute-start(f32[16,64,128]{2,1,0:T(8,128)S(1)} %get-tuple-element.25), channel_id=1, source_target_pairs={{0,1},{1,2},{2,3},{3,4},{4,5},{5,6},{6,7},{7,8},{8,9},{9,10},{10,1... | collective-permute-start | bytes 1572872 | tf_op jit(solution)/shard_map/ppermute | solution.py:469
  5.2 0.7 %copy-start.2 = (s32[1,3]{1,0:T(1,128)S(1)}, s32[1,3]{1,0:T(1,128)}, u32[]{:S(2)}) copy-start(s32[1,3]{1,0:T(1,128)} %lev.1) | copy-start | bytes 40
  5.8 36.5 %copy-start = (bf16[128,128]{1,0:T(8,128)(2,1)S(1)}, bf16[128,128]{1,0:T(8,128)(2,1)}, u32[]{:S(2)}) copy-start(bf16[128,128]{1,0:T(8,128)(2,1)} %constant.30.clone.dz) | copy-start | bytes 98308
  5.8 36.5 %copy-start.1 = (bf16[64,192]{1,0:T(8,128)(2,1)S(1)}, bf16[64,192]{1,0:T(8,128)(2,1)}, u32[]{:S(2)}) copy-start(bf16[64,192]{1,0:T(8,128)(2,1)} %constant.29.clone.dy3) | copy-start | bytes 73732
  35.6 6.7 %collective-permute-start.2 = (f32[16,128]{1,0:T(8,128)S(1)}, f32[16,128]{1,0:T(8,128)S(1)}, u32[]{:S(2)}, u32[]{:S(2)}) collective-permute-start(f32[16,128]{1,0:T(8,128)S(1)} %slice.4), channel_id=1, source_target_pairs={{0,1},{1,0},{2,3},{3,2},{4,5},{5,4},{6,7},{7,6},{8,9},{9,8},{10,11... | collective-permute-start | bytes 24584 | tf_op jit(solution)/shard_map/ppermute | solution.py:476

commit v4 on v3

--- a/solution.py
+++ b/solution.py
@@ -67,23 +67,34 @@
 
 
 def staircase():
-    widths = {0: SPAN, 1: SPAN - 1, 2: SPAN - 2, 3: SPAN - 3, 4: SPAN - 3}
-    blocks = []
-    place = 0
-    for plane, left in widths.items():
+    spare = {0: SPAN, 1: SPAN - 1, 2: SPAN - 2, 3: SPAN - 3, 4: SPAN - 3}
+    summed, kept = [], []
+    for plane, left in spare.items():
         for extra in range(left + 1):
+            whole = 1 << (LOW + left - extra)
+            half = whole // 2 if extra < left else 0
             groups = range(1 << (extra - 1), 1 << extra) if extra else range(1)
             for group in groups:
-                width = 1 << (LOW + left - extra)
-                blocks.append((plane, group, width, place // 128, place % 128))
-                assert place % 128 + width <= 128
-                place += width
-    return blocks, -(-place // 128)
+                if half:
+                    summed.append((plane, group, 0, half))
+                kept.append((plane, group, half, whole - half))
+    blocks = []
+    for base, pieces in ((0, summed), (1, kept)):
+        place = 0
+        for piece in pieces:
+            assert place % 128 + piece[3] <= 128
+            blocks.append((*piece, base + place // 128, place % 128))
+            place += piece[3]
+        assert base or place <= 128
+    return blocks, 1 + max(b[4] for b in blocks)
 
 
 BLOCKS, TILES = staircase()
 NEED = (LOW, LOW + 1, LOW + 2, LOW + 3, LOW + 3)
-SHARED = 1 + max(b[3] for b in BLOCKS if b[0] < 2)
+
+
+def shifted(value, lanes):
+    return pltpu.roll(value, lanes % 128, 1) if lanes % 128 else value
 
 
 def split3(x):
@@ -158,8 +169,8 @@
     lane = lax.broadcasted_iota(jnp.int32, (8, 128), 1)
     groups_y = lax.shift_left(1, level_y - LOW)
     width_z = lax.shift_left(1, level_z)
-    for b, (plane, group, width, _, _) in enumerate(BLOCKS):
-        keep = (lane < jnp.minimum(width_z, width)) & (group < groups_y) & (level_x >= NEED[plane])
+    for b, (plane, group, source, width, _, _) in enumerate(BLOCKS):
+        keep = (lane >= source) & (lane < jnp.minimum(width_z, source + width)) & (group < groups_y) & (level_x >= NEED[plane])
         kept = jnp.where(keep, 1.0, 0.0)
         marks[b] = kept
         marks[len(BLOCKS) + b] = weight * kept
@@ -224,7 +235,7 @@
     out[...] = lanes_dot(jnp.concatenate(planes, axis=0), hz[...]).reshape(out.shape)
 
 
-def edge_kernel(f_in, c_in, cl_in, old_l, old_r, ends, marks, hy3, hz, left, right, out, f_new, c_new, cl_new, nodal):
+def edge_kernel(f_in, c_in, cl_in, old_l, old_r, ends, marks, hy3, hz, left, right, out, stay, f_new, c_new, cl_new, nodal):
     fresh = set()
 
     def take(i):
@@ -280,10 +291,10 @@
                 step_rows(rights[k], take if k else take_r, put, coef_at, first_y)
 
     hierarchize([take(n * GAP) for n in range(NODES)], hy3, hz, nodal)
-    finish(marks, nodal, out)
-
-
-def finish(marks, nodal, out):
+    finish(marks, nodal, out, stay)
+
+
+def finish(marks, nodal, out, stay):
     swapped = marks[2 * len(BLOCKS)] > 0.5
 
     def planes_of(group):
@@ -300,36 +311,33 @@
 
     cache = {}
     tiles = [jnp.zeros((8, 128), jnp.float32)] * TILES
-    for b, (plane, group, width, tile, first) in enumerate(BLOCKS):
+    for b, (plane, group, source, width, tile, first) in enumerate(BLOCKS):
         if group not in cache:
             cache[group] = planes_of(group)
         value = marks[len(BLOCKS) + b] * cache[group][plane]
-        tiles[tile] = tiles[tile] + (pltpu.roll(value, first, 1) if first else value)
+        tiles[tile] = tiles[tile] + shifted(value, first - source)
     for member in range(out.shape[0]):
-        for tile in range(TILES):
-            out[member, 8 * tile : 8 * tile + 8] = tiles[tile]
+        out[member] = tiles[0]
+    for tile in range(1, TILES):
+        stay[tile - 1] = tiles[tile]
 
 
 def spread_kernel(marks, mine, other, dy3, dz, out, held, sem):
     swapped = marks[2 * len(BLOCKS), 0:1] > 0.5
-    own = [mine[8 * t : 8 * t + 8] for t in range(TILES)]
-    theirs = [other[8 * t : 8 * t + 8] for t in range(SHARED)]
     zero = jnp.zeros((8, 128), jnp.float32)
     planes = [[zero] * 8 for _ in range(5)]
     outer_other = [zero] * 8
-    for b, (plane, group, width, tile, first) in enumerate(BLOCKS):
-
-        def pick(source):
-            value = pltpu.roll(source, 128 - first, 1) if first else source
-            return marks[b] * value
-
+    for b, (plane, group, source, width, tile, first) in enumerate(BLOCKS):
+
+        def pick(value):
+            return marks[b] * shifted(value, source - first)
+
+        if plane == 1:
+            planes[1][group] += pick(mine[tile] + other[tile])
+        else:
+            planes[plane][group] += pick(mine[tile])
         if plane == 0:
-            planes[0][group] = pick(own[tile])
-            outer_other[group] = pick(theirs[tile])
-        elif plane == 1:
-            planes[1][group] = pick(own[tile] + theirs[tile])
-        else:
-            planes[plane][group] = pick(own[tile])
+            outer_other[group] += pick(other[tile])
     wide = []
     outer = jnp.concatenate(planes[0], axis=0)
     middle = 0.5 * (outer + jnp.concatenate(outer_other, axis=0)) + jnp.concatenate(planes[1], axis=0)
@@ -429,9 +437,12 @@
 def edge(members, state, left, right, interpret=False):
     return pl.pallas_call(
         edge_kernel,
-        out_shape=jax.ShapeDtypeStruct((members, 8 * TILES, 128), jnp.float32),
+        out_shape=(
+            jax.ShapeDtypeStruct((members, 8, 128), jnp.float32),
+            jax.ShapeDtypeStruct((TILES - 1, 8, 128), jnp.float32),
+        ),
         in_specs=[VMEM] * 11,
-        out_specs=VMEM,
+        out_specs=(VMEM, VMEM),
         scratch_shapes=[
             pltpu.VMEM((TALL, 8, 8, 128), jnp.float32),
             pltpu.VMEM((5, TALL, 8, 8, 128), jnp.float32),
@@ -470,11 +481,11 @@
     right = lax.ppermute(going_down, "space", down)
     odd = (lax.axis_index("space") % 2).astype(jnp.int32)[None]
     state = inner(levels, coefs, odd, den, kap)
-    sent = edge(grid, state, left, right)
+    sent, stay = edge(grid, state, left, right)
     got = lax.all_to_all(sent, "grid", split_axis=0, concat_axis=0, tiled=True)
-    total = jnp.sum(got, axis=0)
-    other = lax.ppermute(total[: 8 * SHARED], "space", pair)
-    return spread(state[6], total, other)[None]
+    mine = jnp.concatenate([jnp.sum(got, axis=0, keepdims=True), stay], axis=0)
+    other = lax.ppermute(mine, "space", pair)
+    return spread(state[6], mine, other)[None]
 
 
 def solution(mesh):

time: 44 us -> 43.3 us (0.984)
  blocking collectives: 20.2 us -> 19.5 us
    all_to_all x1, blocking collectives: 20.2 us -> 19.5 us  [local(): got = lax.all_to_all(sent, 'grid', split_axis=0, concat_axis=0, tiled=True)]
where the time goes in v4:
time: 43.3 us; the launch traced here: 43.1 us
  blocking collectives  19.5 us (45%)
  Pallas kernels  12.2 us (28%)
  starting transfers between devices  9.21 us (21%)
  waiting for transfers between devices  0.84 us (2%)
  between operations  0.71 us (2%)
  local copies, waits for them, and re-layouts  0.66 us (2%)
    all_to_all x1, blocking collectives, local(): got = lax.all_to_all(sent, 'grid', split_axis=0, concat_axis=0, tiled=True)  19.5 us
    pallas_call x1, Pallas kernels, inner(): pl.pallas_call(inner_kernel, out_shape=(rows, rows_shape(5, ROWS), jax.Sh...  6.07 us
    ppermute x1, starting transfers between devices, local(): other = lax.ppermute(mine, 'space', pair)  5.93 us
    pallas_call x1, Pallas kernels, edge(): pl.pallas_call(edge_kernel, out_shape=(jax.ShapeDtypeStruct((members, 8,...  3.4 us
    ppermute x1, starting transfers between devices, local(): right = lax.ppermute(going_down, 'space', down)  3.28 us
    pallas_call x1, Pallas kernels, spread(): pl.pallas_call(spread_kernel, out_shape=jax.ShapeDtypeStruct((ROWS, NY, N...  1.46 us
    pallas_call x1, Pallas kernels, send(): pl.pallas_call(send_kernel, out_shape=(jax.ShapeDtypeStruct((2 * LEFT, NY...  1.24 us
  transfers between devices with their start and end apart: 3, of which 1 were waited for; matrix products, arithmetic and copies ran while one was open for 0% of the time, Pallas kernels for 14%

profile of v4, /device:TPU:1, one launch (start us, length us, event | category | flops | bytes accessed | tf_op | source)
XLA Modules:
  0.0 43.1 jit_solution(14224149222992794593)
XLA Ops:
  0.0 1.2 %send.1 = (f32[16,64,128]{2,1,0:T(8,128)S(1)}, f32[18,64,128]{2,1,0:T(8,128)S(1)}) custom-call(f32[32,64,128]{2,1,0:T(8,128)} %bitcast.5, f32[32,64,128]{2,1,0:T(8,128)} %bitcast.7), custom_call_target="tpu_custom_call" | custom-call | tf_op jit(solution)/shard_map/send/pallas_call | solution.py:395
  1.2 3.3 %collective-permute-start.1 = (f32[18,64,128]{2,1,0:T(8,128)S(1)}, f32[18,64,128]{2,1,0:T(8,128)S(1)}, u32[]{:S(2)}, u32[]{:S(2)}) collective-permute-start(f32[18,64,128]{2,1,0:T(8,128)S(1)} %get-tuple-element.28), channel_id=1, source_target_pairs={{1,0},{2,1},{3,2},{4,3},{5,4},{6,5},{7,6},{8,7},{9,8},{10,9},{11,1... | collective-permute-start | bytes 1769480 | tf_op jit(solution)/shard_map/ppermute | solution.py:481
  4.5 0.0 collective-permute-start
  5.2 0.0 copy-start.2
  5.2 0.6 %copy-done.2 = s32[1,3]{1,0:T(1,128)S(1)} copy-done((s32[1,3]{1,0:T(1,128)S(1)}, s32[1,3]{1,0:T(1,128)}, u32[]{:S(2)}) %copy-start.2) | copy-done | bytes 36
  5.8 0.0 copy-start
  5.8 0.0 copy-start.1
  5.8 6.1 %inner.1 = (f32[32,8,8,128]{3,2,1,0:T(8,128)S(1)}, f32[5,32,8,8,128]{4,3,2,1,0:T(8,128)S(1)}, f32[32,8,128]{2,1,0:T(8,128)S(1)}, f32[4,8,8,128]{3,2,1,0:T(8,128)...) custom-call(s32[1,3]{1,0:T(1,128)S(1)} %copy-done.2, ...), custom_call_target="tpu_custom_call" | custom-call | flops 20000000 | bytes 8000000 | tf_op jit(solution)/shard_map/inner/pallas_call | solution.py:413
  11.9 0.0 collective-permute-done.left
  11.9 0.0 collective-permute-done.1.right
  11.9 3.4 %edge.1 = (f32[16,8,128]{2,1,0:T(8,128)S(1)}, f32[2,8,128]{2,1,0:T(8,128)S(1)}) custom-call(f32[32,8,8,128]{3,2,1,0:T(8,128)S(1)} %get-tuple-element.19.f_in, f32[5,32,8,8,128]{4,3,2,1,0:T(8,128)S(1)} %get-tuple-element.20.c_in, f32[32,8,128]{2,1,0:T(8,128)S(1)} %get-tuple-element.21.cl_in, f32[4,8,8,128]{3,2,1,0:T(8,128)S(1)} %get-tuple-element.22.old_l, ...), custom_call_target="tpu_custom_call" | custom-call | tf_op jit(solution)/shard_map/edge/pallas_call | solution.py:438
  15.4 19.5 %all_to_all.5 = f32[16,8,128]{2,1,0:T(8,128)S(1)} all-to-all(f32[16,8,128]{2,1,0:T(8,128)S(1)} %get-tuple-element.29), channel_id=1, replica_groups=mesh['grid'=16,'space'=16] {'grid'}, dimensions={0} | all-to-all | bytes 131072 | tf_op jit(solution)/shard_map/all_to_all | solution.py:485
  34.9 5.9 %collective-permute-start.2 = (f32[3,8,128]{2,1,0:T(8,128)S(1)}, f32[3,8,128]{2,1,0:T(8,128)S(1)}, u32[]{:S(2)}, u32[]{:S(2)}) collective-permute-start(f32[3,8,128]{2,1,0:T(8,128)S(1)} %pad_maximum_fusion.mine), channel_id=1, source_target_pairs={{0,1},{1,0},{2,3},{3,2},{4,5},{5,4},{6,7},{7,6},{8,9},{9,8},{10,11... | collective-permute-start | bytes 36872 | tf_op jit(solution)/shard_map/ppermute | solution.py:487
  40.8 0.8 %collective-permute-done.2.other = f32[3,8,128]{2,1,0:T(8,128)S(1)} collective-permute-done((f32[3,8,128]{2,1,0:T(8,128)S(1)}, f32[3,8,128]{2,1,0:T(8,128)S(1)}, u32[]{:S(2)}, u32[]{:S(2)}) %collective-permute-start.2) | collective-permute-done | bytes 12320 | tf_op jit(solution)/shard_map/ppermute | solution.py:487
  41.6 0.0 copy-done
  41.6 0.0 copy-done.1
  41.6 1.5 %spread.1 = f32[32,64,128]{2,1,0:T(8,128)} custom-call(f32[47,8,128]{2,1,0:T(8,128)S(1)} %get-tuple-element.18.marks, f32[3,8,128]{2,1,0:T(8,128)S(1)} %pad_maximum_fusion.mine, f32[3,8,128]{2,1,0:T(8,128)S(1)} %collective-permute-done.2.other, bf16[64,192]{1,0:T(8,128)(2,1)S(1)} %copy-done.1, bf16[128,128]{1,0:T(8,128)(2,1)S(1)} %copy-done), custom_call_target="tpu_custom_call" | custom-call | tf_op jit(solution)/shard_map/spread/pallas_call | solution.py:460
  (2 shorter events, 0.0 us)
Async XLA Ops:
  1.2 10.7 %collective-permute-start.1 = (f32[18,64,128]{2,1,0:T(8,128)S(1)}, f32[18,64,128]{2,1,0:T(8,128)S(1)}, u32[]{:S(2)}, u32[]{:S(2)}) collective-permute-start(f32[18,64,128]{2,1,0:T(8,128)S(1)} %get-tuple-element.28), channel_id=1, source_target_pairs={{1,0},{2,1},{3,2},{4,3},{5,4},{6,5},{7,6},{8,7},{9,8},{10,9},{11,1... | collective-permute-start | bytes 1769480 | tf_op jit(solution)/shard_map/ppermute | solution.py:481
  4.5 7.4 %collective-permute-start = (f32[16,64,128]{2,1,0:T(8,128)S(1)}, f32[16,64,128]{2,1,0:T(8,128)S(1)}, u32[]{:S(2)}, u32[]{:S(2)}) collective-permute-start(f32[16,64,128]{2,1,0:T(8,128)S(1)} %get-tuple-element.27), channel_id=1, source_target_pairs={{0,1},{1,2},{2,3},{3,4},{4,5},{5,6},{6,7},{7,8},{8,9},{9,10},{10,1... | collective-permute-start | bytes 1572872 | tf_op jit(solution)/shard_map/ppermute | solution.py:480
  5.2 0.7 %copy-start.2 = (s32[1,3]{1,0:T(1,128)S(1)}, s32[1,3]{1,0:T(1,128)}, u32[]{:S(2)}) copy-start(s32[1,3]{1,0:T(1,128)} %lev.1) | copy-start | bytes 40
  5.8 35.8 %copy-start = (bf16[128,128]{1,0:T(8,128)(2,1)S(1)}, bf16[128,128]{1,0:T(8,128)(2,1)}, u32[]{:S(2)}) copy-start(bf16[128,128]{1,0:T(8,128)(2,1)} %constant.30.clone.dz) | copy-start | bytes 98308
  5.8 35.8 %copy-start.1 = (bf16[64,192]{1,0:T(8,128)(2,1)S(1)}, bf16[64,192]{1,0:T(8,128)(2,1)}, u32[]{:S(2)}) copy-start(bf16[64,192]{1,0:T(8,128)(2,1)} %constant.29.clone.dy3) | copy-start | bytes 73732
  34.9 6.8 %collective-permute-start.2 = (f32[3,8,128]{2,1,0:T(8,128)S(1)}, f32[3,8,128]{2,1,0:T(8,128)S(1)}, u32[]{:S(2)}, u32[]{:S(2)}) collective-permute-start(f32[3,8,128]{2,1,0:T(8,128)S(1)} %pad_maximum_fusion.mine), channel_id=1, source_target_pairs={{0,1},{1,0},{2,3},{3,2},{4,5},{5,4},{6,7},{7,6},{8,9},{9,8},{10,11... | collective-permute-start | bytes 36872 | tf_op jit(solution)/shard_map/ppermute | solution.py:487

commit v5 on v4

--- a/solution.py
+++ b/solution.py
@@ -7,6 +7,7 @@
 from jax.experimental import pallas as pl
 from jax.experimental.pallas import tpu as pltpu
 from jax.sharding import PartitionSpec as P
+
 
 ITERS = 8
 LOW = 3
@@ -97,6 +98,10 @@
     return pltpu.roll(value, lanes % 128, 1) if lanes % 128 else value
 
 
+def parity():
+    return lax.rem(lax.axis_index("space"), 2)
+
+
 def split3(x):
     hi = x.astype(jnp.bfloat16)
     rest = x - hi.astype(jnp.float32)
@@ -163,7 +168,7 @@
     return [r for r in spans if len(r)]
 
 
-def write_marks(lev, coef, odd, marks):
+def write_marks(lev, coef, marks):
     level_x, level_y, level_z = lev[0, 0], lev[0, 1], lev[0, 2]
     weight = coef[0].astype(jnp.float32)
     lane = lax.broadcasted_iota(jnp.int32, (8, 128), 1)
@@ -174,10 +179,10 @@
         kept = jnp.where(keep, 1.0, 0.0)
         marks[b] = kept
         marks[len(BLOCKS) + b] = weight * kept
-    marks[2 * len(BLOCKS)] = jnp.full((8, 128), odd[0].astype(jnp.float32))
-
-
-def inner_kernel(lev, coef, odd, den, kap, hy3, hz, f_ref, c_ref, cl_ref, old_l, old_r, ends, marks, hy3_v, hz_v, den_v, kap_v, sem, sem_w):
+    marks[2 * len(BLOCKS)] = jnp.full((8, 128), parity() * 1.0, jnp.float32)
+
+
+def inner_kernel(lev_h, coef, den, kap, hy3, hz, f_ref, c_ref, cl_ref, old_l, old_r, ends, marks, hy3_v, hz_v, den_v, kap_v, lev, sem, sem_w):
     parts = ROWS // CHUNK
 
     def copies(part):
@@ -191,9 +196,9 @@
         for copy in copies(part):
             copy.start()
     weights = [pltpu.make_async_copy(hy3, hy3_v, sem_w.at[0]), pltpu.make_async_copy(hz, hz_v, sem_w.at[1])]
-    for copy in weights:
+    scalars = [pltpu.make_async_copy(lev_h, lev, sem_w.at[2])]
+    for copy in weights + scalars:
         copy.start()
-    write_marks(lev, coef, odd, marks)
     before = jnp.zeros((8, 8, 128), jnp.float32)
     for part in range(parts):
         for copy in copies(part):
@@ -226,6 +231,9 @@
 
             step_rows(rows, lambda i: f_ref[i], put, lambda a, i: c_ref[a, i], lambda i: cl_ref[i], keep)
     old_r[ITERS - 1] = f_ref[ROWS - 1 - ITERS]
+    for copy in scalars:
+        copy.wait()
+    write_marks(lev, coef, marks)
     for copy in weights:
         copy.wait()
 
@@ -235,7 +243,8 @@
     out[...] = lanes_dot(jnp.concatenate(planes, axis=0), hz[...]).reshape(out.shape)
 
 
-def edge_kernel(f_in, c_in, cl_in, old_l, old_r, ends, marks, hy3, hz, left, right, out, stay, f_new, c_new, cl_new, nodal):
+def one_end(is_left, state, halo, f_new, c_new, cl_new):
+    f_in, c_in, cl_in, old_l, old_r, ends = state
     fresh = set()
 
     def take(i):
@@ -251,46 +260,72 @@
     def first_y(i):
         return cl_in[i] if 0 <= i < ROWS else cl_new[i + LEFT]
 
-    def prepare(source, first, count, edge_row, edge_k):
-        before = None
-        for t in range(count):
-            i = first + t
-            k = fetch(source, count + t)
-            f_new[i + LEFT] = fetch(source, t)
-            at = i + LEFT
-            c_new[1, at], c_new[2, at], c_new[3, at], c_new[4, at], cl_new[at] = row_coefs(k)
-            if before is not None:
-                c_new[0, i - 1 + LEFT] = 0.5 * (before + k)
-            if i == edge_row + 1:
-                c_new[0, edge_row + LEFT] = 0.5 * (edge_k + k)
-            if i == edge_row:
-                c_new[0, edge_row + LEFT] = 0.5 * (edge_k + k)
-            before = k
-
-    prepare(left, -LEFT, LEFT, -1, ends[0])
-    prepare(right, ROWS, RIGHT, ROWS - 1, ends[1])
+    skip = RIGHT - LEFT if is_left else 0
+    first, count = (-LEFT, LEFT) if is_left else (ROWS, RIGHT)
+    before = None if is_left else ends[1]
+    for t in range(count):
+        at = first + t + LEFT
+        k = fetch(halo, RIGHT + skip + t)
+        f_new[at] = fetch(halo, skip + t)
+        c_new[1, at], c_new[2, at], c_new[3, at], c_new[4, at], cl_new[at] = row_coefs(k)
+        if before is not None:
+            c_new[0, at - 1] = 0.5 * (before + k)
+        before = k
+    if is_left:
+        c_new[0, LEFT - 1] = 0.5 * (before + ends[0])
 
     for step in range(1, ITERS + 1):
         reach = ITERS - step
-        if step <= 4:
-            lefts, rights = [range(-reach, step)], [range(ROWS - step, ROWS + reach + 1)]
+        if is_left:
+            spans = [range(-reach, step if step <= 4 else reach + 1)]
+        elif step <= 4:
+            spans = [range(ROWS - step, ROWS + reach + 1)]
         else:
-            lefts = [range(-reach, reach + 1)]
-            rights = [range(ROWS - step, ROWS - step + 1), range(ROWS - reach, ROWS + reach + 1)]
-
-        def take_l(i, step=step):
-            return old_l[step - 1] if i == step and step <= 4 else take(i)
-
-        def take_r(i, step=step):
+            spans = [range(ROWS - step, ROWS - step + 1), range(ROWS - reach, ROWS + reach + 1)]
+
+        def take_old(i, step=step):
+            if is_left:
+                return old_l[step - 1] if i == step and step <= 4 else take(i)
             return old_r[step - 1] if i == ROWS - 1 - step else take(i)
 
-        for k in range(max(len(lefts), len(rights))):
-            if k < len(lefts):
-                step_rows(lefts[k], take_l, put, coef_at, first_y)
-            if k < len(rights):
-                step_rows(rights[k], take if k else take_r, put, coef_at, first_y)
-
-    hierarchize([take(n * GAP) for n in range(NODES)], hy3, hz, nodal)
+        for n, rows in enumerate(spans):
+            step_rows(rows, take if n else take_old, put, coef_at, first_y)
+    return take
+
+
+def chip_kernel(*refs):
+    state, halo, out, work = refs[:6], refs[6], refs[7], refs[8:]
+
+    @pl.when(parity() == 0)
+    def _():
+        take = one_end(False, state, halo, *work)
+        out[0] = take(3 * GAP)
+        out[1] = take(4 * GAP)
+
+    @pl.when(parity() == 1)
+    def _():
+        out[0] = one_end(True, state, halo, *work)(0)
+
+
+def cross_kernel(*refs):
+    state, (marks, hy3, hz, near, halo, out, stay), work, nodes, nodal = refs[:6], refs[6:13], refs[13:16], refs[16], refs[17]
+    for n in (1, 2):
+        nodes[n] = state[0][n * GAP]
+
+    @pl.when(parity() == 0)
+    def _():
+        nodes[0] = one_end(True, state, halo, *work)(0)
+        nodes[3] = near[0]
+        nodes[4] = near[1]
+
+    @pl.when(parity() == 1)
+    def _():
+        take = one_end(False, state, halo, *work)
+        nodes[0] = near[0]
+        nodes[3] = take(3 * GAP)
+        nodes[4] = take(4 * GAP)
+
+    hierarchize([nodes[n] for n in range(NODES)], hy3, hz, nodal)
     finish(marks, nodal, out, stay)
 
 
@@ -366,13 +401,14 @@
 FAR = pl.BlockSpec(memory_space=pltpu.HBM)
 
 
-def send_kernel(den, kap, up, down, sem):
-    copies = [
-        pltpu.make_async_copy(den.at[pl.ds(ROWS - LEFT, LEFT)], up.at[pl.ds(0, LEFT)], sem.at[0]),
-        pltpu.make_async_copy(kap.at[pl.ds(ROWS - LEFT, LEFT)], up.at[pl.ds(LEFT, LEFT)], sem.at[1]),
-        pltpu.make_async_copy(den.at[pl.ds(0, RIGHT)], down.at[pl.ds(0, RIGHT)], sem.at[2]),
-        pltpu.make_async_copy(kap.at[pl.ds(0, RIGHT)], down.at[pl.ds(RIGHT, RIGHT)], sem.at[3]),
-    ]
+def send_kernel(den, kap, cross, chip, sem):
+    low = (ROWS - RIGHT) * parity()
+    copies = []
+    for n, (out, start) in enumerate(((cross, low), (chip, ROWS - RIGHT - low))):
+        for m, source in enumerate((den, kap)):
+            copies.append(
+                pltpu.make_async_copy(source.at[pl.ds(start, RIGHT)], out.at[pl.ds(m * RIGHT, RIGHT)], sem.at[n, m])
+            )
     for copy in copies:
         copy.start()
     for copy in copies:
@@ -395,19 +431,19 @@
     return pl.pallas_call(
         send_kernel,
         out_shape=(
-            jax.ShapeDtypeStruct((2 * LEFT, NY, NZ), jnp.float32),
+            jax.ShapeDtypeStruct((2 * RIGHT, NY, NZ), jnp.float32),
             jax.ShapeDtypeStruct((2 * RIGHT, NY, NZ), jnp.float32),
         ),
         in_specs=[FAR] * 2,
         out_specs=(VMEM, VMEM),
-        scratch_shapes=[pltpu.SemaphoreType.DMA((4,))],
+        scratch_shapes=[pltpu.SemaphoreType.DMA((2, 2))],
         compiler_params=params(8 * 1024 * 1024),
         interpret=interpret,
         name="send",
     )(far(den), far(kap))
 
 
-def inner(levels, coefs, odd, den, kap, interpret=False):
+def inner(levels, coefs, den, kap, interpret=False):
     rows = rows_shape(ROWS)
     hy3, hz, _, _ = constants()
     return pl.pallas_call(
@@ -423,36 +459,57 @@
             jax.ShapeDtypeStruct(hy3.shape, jnp.bfloat16),
             jax.ShapeDtypeStruct(hz.shape, jnp.bfloat16),
         ),
-        in_specs=[SMEM] * 3 + [FAR] * 4,
+        in_specs=[FAR, SMEM] + [FAR] * 4,
         out_specs=(VMEM,) * 9,
         scratch_shapes=[pltpu.VMEM((ROWS, NY, NZ), jnp.float32)] * 2
-        + [pltpu.SemaphoreType.DMA((2, ROWS // CHUNK)), pltpu.SemaphoreType.DMA((2,))],
+        + [
+            pltpu.SMEM((1, 3), jnp.int32),
+            pltpu.SemaphoreType.DMA((2, ROWS // CHUNK)),
+            pltpu.SemaphoreType.DMA((3,)),
+        ],
         compiler_params=params(),
         cost_estimate=pl.CostEstimate(flops=20_000_000, bytes_accessed=8_000_000, transcendentals=0),
         interpret=interpret,
         name="inner",
-    )(levels, coefs, odd, far(den), far(kap), far(jnp.asarray(hy3, jnp.bfloat16)), far(jnp.asarray(hz, jnp.bfloat16)))
-
-
-def edge(members, state, left, right, interpret=False):
+    )(far(levels), coefs, far(den), far(kap), far(jnp.asarray(hy3, jnp.bfloat16)), far(jnp.asarray(hz, jnp.bfloat16)))
+
+
+def work():
+    return [
+        pltpu.VMEM((TALL, 8, 8, 128), jnp.float32),
+        pltpu.VMEM((5, TALL, 8, 8, 128), jnp.float32),
+        pltpu.VMEM((TALL, 8, 128), jnp.float32),
+    ]
+
+
+def chip_end(state, halo, interpret=False):
     return pl.pallas_call(
-        edge_kernel,
+        chip_kernel,
+        out_shape=rows_shape(2),
+        in_specs=[VMEM] * 7,
+        out_specs=VMEM,
+        scratch_shapes=work(),
+        compiler_params=params(),
+        cost_estimate=pl.CostEstimate(flops=10_000_000, bytes_accessed=4_000_000, transcendentals=0),
+        interpret=interpret,
+        name="chip_end",
+    )(*state[:6], halo)
+
+
+def cross_end(members, state, near, halo, interpret=False):
+    return pl.pallas_call(
+        cross_kernel,
         out_shape=(
             jax.ShapeDtypeStruct((members, 8, 128), jnp.float32),
             jax.ShapeDtypeStruct((TILES - 1, 8, 128), jnp.float32),
         ),
         in_specs=[VMEM] * 11,
         out_specs=(VMEM, VMEM),
-        scratch_shapes=[
-            pltpu.VMEM((TALL, 8, 8, 128), jnp.float32),
-            pltpu.VMEM((5, TALL, 8, 8, 128), jnp.float32),
-            pltpu.VMEM((TALL, 8, 128), jnp.float32),
-            pltpu.VMEM((NODES, 8, 8, 128), jnp.float32),
-        ],
+        scratch_shapes=work() + [pltpu.VMEM((NODES, 8, 8, 128), jnp.float32)] * 2,
         compiler_params=params(),
         interpret=interpret,
-        name="edge",
-    )(*state, left, right)
+        name="cross_end",
+    )(*state, near, halo)
 
 
 def spread(marks, mine, other, interpret=False):
@@ -473,15 +530,14 @@
     den, kap = density[0], kappa[0]
     space, grid = lax.axis_size("space"), lax.axis_size("grid")
     assert den.shape == (ROWS, NY, NZ) and space * ROWS == 512
-    up = [(i, (i + 1) % space) for i in range(space)]
-    down = [(j, i) for i, j in up]
     pair = [(i, i ^ 1) for i in range(space)]
-    going_up, going_down = send(den, kap)
-    left = lax.ppermute(going_up, "space", up)
-    right = lax.ppermute(going_down, "space", down)
-    odd = (lax.axis_index("space") % 2).astype(jnp.int32)[None]
-    state = inner(levels, coefs, odd, den, kap)
-    sent, stay = edge(grid, state, left, right)
+    other_chip = [(i, (i + 1 if i % 2 else i - 1) % space) for i in range(space)]
+    to_cross, to_chip = send(den, kap)
+    cross = lax.ppermute(to_cross, "space", other_chip)
+    chip = lax.ppermute(to_chip, "space", pair)
+    state = inner(levels, coefs, den, kap)
+    near = chip_end(state, chip)
+    sent, stay = cross_end(grid, state, near, cross)
     got = lax.all_to_all(sent, "grid", split_axis=0, concat_axis=0, tiled=True)
     mine = jnp.concatenate([jnp.sum(got, axis=0, keepdims=True), stay], axis=0)
     other = lax.ppermute(mine, "space", pair)

time: 43.3 us -> 39.8 us (0.919)
  starting transfers between devices: 9.21 us -> 6.58 us
  waiting for transfers between devices: 0.84 us -> 2.87 us
  blocking collectives: 19.5 us -> 18 us
  Pallas kernels: 12.2 us -> 11.4 us
  local copies, waits for them, and re-layouts: 0.66 us -> 0.01 us
    ppermute x1, starting transfers between devices: 5.93 us -> 3.29 us  [local(): other = lax.ppermute(mine, 'space', pair)]
    ppermute x2, waiting for transfers between devices: 0.01 us -> 2.03 us  [the longest x1 2.03 us: local(): cross = lax.ppermute(to_cross, 'space', other_chip)]
    all_to_all x1, blocking collectives: 19.5 us -> 18 us  [local(): got = lax.all_to_all(sent, 'grid', split_axis=0, concat_axis=0, tiled=True)]
    unnamed x6 -> x4, local copies, waits for them, and re-layouts: 0.66 us -> 0.01 us
    pallas_call x1, Pallas kernels: 6.07 us -> 5.63 us  [inner(): pl.pallas_call(inner_kernel, out_shape=(rows, rows_shape(5, ROWS), jax.Sh...]
    pallas_call x2 -> x3, Pallas kernels: 4.64 us -> 4.33 us  [the longest x1 1.83 us: cross_end(): pl.pallas_call(cross_kernel, out_shape=(jax.ShapeDtypeStruct((members, 8,...]
  transfers between devices with their start and end apart: 3 -> 3, of which waited for: 1 -> 2; matrix products, arithmetic and copies ran while one was open for 0% -> 0% of each run, Pallas kernels for 14% -> 17%
where the time goes in v5:
time: 39.8 us; the launch traced here: 39.6 us
  blocking collectives  18 us (45%)
  Pallas kernels  11.4 us (29%)
  starting transfers between devices  6.58 us (17%)
  waiting for transfers between devices  2.87 us (7%)
  between operations  0.71 us (2%)
    all_to_all x1, blocking collectives, local(): got = lax.all_to_all(sent, 'grid', split_axis=0, concat_axis=0, tiled=True)  18 us
    pallas_call x1, Pallas kernels, inner(): pl.pallas_call(inner_kernel, out_shape=(rows, rows_shape(5, ROWS), jax.Sh...  5.63 us
    ppermute x1, starting transfers between devices, local(): other = lax.ppermute(mine, 'space', pair)  3.29 us
    ppermute x1, starting transfers between devices, local(): chip = lax.ppermute(to_chip, 'space', pair)  3.29 us
    ppermute x1, waiting for transfers between devices, local(): cross = lax.ppermute(to_cross, 'space', other_chip)  2.03 us
    pallas_call x1, Pallas kernels, cross_end(): pl.pallas_call(cross_kernel, out_shape=(jax.ShapeDtypeStruct((members, 8,...  1.83 us
    pallas_call x1, Pallas kernels, spread(): pl.pallas_call(spread_kernel, out_shape=jax.ShapeDtypeStruct((ROWS, NY, N...  1.46 us
    pallas_call x1, Pallas kernels, send(): pl.pallas_call(send_kernel, out_shape=(jax.ShapeDtypeStruct((2 * RIGHT, N...  1.26 us
  transfers between devices with their start and end apart: 3, of which 2 were waited for; matrix products, arithmetic and copies ran while one was open for 0% of the time, Pallas kernels for 17%

profile of v5, /device:TPU:1, one launch (start us, length us, event | category | flops | bytes accessed | tf_op | source)
XLA Modules:
  0.0 39.6 jit_solution(17896859082851297802)
XLA Ops:
  0.0 1.3 %send.1 = (f32[18,64,128]{2,1,0:T(8,128)S(1)}, f32[18,64,128]{2,1,0:T(8,128)S(1)}) custom-call(f32[32,64,128]{2,1,0:T(8,128)} %bitcast.4, f32[32,64,128]{2,1,0:T(8,128)} %bitcast.6), custom_call_target="tpu_custom_call" | custom-call | tf_op jit(solution)/shard_map/send/pallas_call | solution.py:431
  1.3 3.3 %collective-permute-start = (f32[18,64,128]{2,1,0:T(8,128)S(1)}, f32[18,64,128]{2,1,0:T(8,128)S(1)}, u32[]{:S(2)}, u32[]{:S(2)}) collective-permute-start(f32[18,64,128]{2,1,0:T(8,128)S(1)} %get-tuple-element.27), channel_id=1, source_target_pairs={{0,1},{1,0},{2,3},{3,2},{4,5},{5,4},{6,7},{7,6},{8,9},{9,8},{10,11... | collective-permute-start | bytes 1769480 | tf_op jit(solution)/shard_map/ppermute | solution.py:537
  4.6 0.0 collective-permute-start.1
  5.2 5.6 %inner.1 = (f32[32,8,8,128]{3,2,1,0:T(8,128)S(1)}, f32[5,32,8,8,128]{4,3,2,1,0:T(8,128)S(1)}, f32[32,8,128]{2,1,0:T(8,128)S(1)}, f32[4,8,8,128]{3,2,1,0:T(8,128)...) custom-call(s32[1,3]{1,0:T(1,128)} %lev_h.1, ...), custom_call_target="tpu_custom_call" | custom-call | flops 20000000 | bytes 8000000 | tf_op jit(solution)/shard_map/inner/pallas_call | solution.py:449
  10.8 0.0 collective-permute-done.refs_6_
  10.9 1.2 %chip_end.1.refs_9_ = f32[2,8,8,128]{3,2,1,0:T(8,128)S(1)} custom-call(f32[32,8,8,128]{3,2,1,0:T(8,128)S(1)} %get-tuple-element.19.refs_0_, f32[5,32,8,8,128]{4,3,2,1,0:T(8,128)S(1)} %get-tuple-element.20.refs_1_, f32[32,8,128]{2,1,0:T(8,128)S(1)} %get-tuple-element.21.refs_2_, f32[4,8,8,128]{3,2,1,0:T(8,128)S(1)} %get-tuple-element.22.refs_3_, ...), custom_call_target="tpu_custom_call" | custom-call | flops 10000000 | bytes 4000000 | tf_op jit(solution)/shard_map/chip_end/pallas_call | solution.py:486
  12.1 0.0 copy-start
  12.1 0.0 copy-start.1
  12.1 2.0 %collective-permute-done.1.refs_10_ = f32[18,64,128]{2,1,0:T(8,128)S(1)} collective-permute-done((f32[18,64,128]{2,1,0:T(8,128)S(1)}, f32[18,64,128]{2,1,0:T(8,128)S(1)}, u32[]{:S(2)}, u32[]{:S(2)}) %collective-permute-start.1) | collective-permute-done | bytes 589856 | tf_op jit(solution)/shard_map/ppermute | solution.py:536
  14.2 1.8 %cross_end.1 = (f32[16,8,128]{2,1,0:T(8,128)S(1)}, f32[2,8,128]{2,1,0:T(8,128)S(1)}) custom-call(f32[32,8,8,128]{3,2,1,0:T(8,128)S(1)} %get-tuple-element.19.refs_0_, f32[5,32,8,8,128]{4,3,2,1,0:T(8,128)S(1)} %get-tuple-element.20.refs_1_, f32[32,8,128]{2,1,0:T(8,128)S(1)} %get-tuple-element.21.refs_2_, f32[4,8,8,128]{3,2,1,0:T(8,128)S(1)} %get-tuple-element.22.refs_3_, ...), custom_call_target="tpu_custom_call" | custom-call | tf_op jit(solution)/shard_map/cross_end/pallas_call | solution.py:500
  16.0 18.0 %all_to_all.5 = f32[16,8,128]{2,1,0:T(8,128)S(1)} all-to-all(f32[16,8,128]{2,1,0:T(8,128)S(1)} %get-tuple-element.29), channel_id=1, replica_groups=mesh['grid'=16,'space'=16] {'grid'}, dimensions={0} | all-to-all | bytes 131072 | tf_op jit(solution)/shard_map/all_to_all | solution.py:541
  34.0 3.3 %collective-permute-start.2 = (f32[3,8,128]{2,1,0:T(8,128)S(1)}, f32[3,8,128]{2,1,0:T(8,128)S(1)}, u32[]{:S(2)}, u32[]{:S(2)}) collective-permute-start(f32[3,8,128]{2,1,0:T(8,128)S(1)} %pad_maximum_fusion.mine), channel_id=1, source_target_pairs={{0,1},{1,0},{2,3},{3,2},{4,5},{5,4},{6,7},{7,6},{8,9},{9,8},{10,11... | collective-permute-start | bytes 36872 | tf_op jit(solution)/shard_map/ppermute | solution.py:543
  37.3 0.8 %collective-permute-done.2.other = f32[3,8,128]{2,1,0:T(8,128)S(1)} collective-permute-done((f32[3,8,128]{2,1,0:T(8,128)S(1)}, f32[3,8,128]{2,1,0:T(8,128)S(1)}, u32[]{:S(2)}, u32[]{:S(2)}) %collective-permute-start.2) | collective-permute-done | bytes 12320 | tf_op jit(solution)/shard_map/ppermute | solution.py:543
  38.2 0.0 copy-done
  38.2 0.0 copy-done.1
  38.2 1.5 %spread.1 = f32[32,64,128]{2,1,0:T(8,128)} custom-call(f32[47,8,128]{2,1,0:T(8,128)S(1)} %get-tuple-element.18.refs_6_.marks, f32[3,8,128]{2,1,0:T(8,128)S(1)} %pad_maximum_fusion.mine, f32[3,8,128]{2,1,0:T(8,128)S(1)} %collective-permute-done.2.other, bf16[64,192]{1,0:T(8,128)(2,1)S(1)} %copy-done.1, bf16[128,128]{1,0:T(8,128)(2,1)S(1)} %copy-done), custom_call_target="tpu_custom_call" | custom-call | tf_op jit(solution)/shard_map/spread/pallas_call | solution.py:517
  (2 shorter events, 0.0 us)
Async XLA Ops:
  1.3 9.6 %collective-permute-start = (f32[18,64,128]{2,1,0:T(8,128)S(1)}, f32[18,64,128]{2,1,0:T(8,128)S(1)}, u32[]{:S(2)}, u32[]{:S(2)}) collective-permute-start(f32[18,64,128]{2,1,0:T(8,128)S(1)} %get-tuple-element.27), channel_id=1, source_target_pairs={{0,1},{1,0},{2,3},{3,2},{4,5},{5,4},{6,7},{7,6},{8,9},{9,8},{10,11... | collective-permute-start | bytes 1769480 | tf_op jit(solution)/shard_map/ppermute | solution.py:537
  4.6 9.6 %collective-permute-start.1 = (f32[18,64,128]{2,1,0:T(8,128)S(1)}, f32[18,64,128]{2,1,0:T(8,128)S(1)}, u32[]{:S(2)}, u32[]{:S(2)}) collective-permute-start(f32[18,64,128]{2,1,0:T(8,128)S(1)} %get-tuple-element.28), channel_id=1, source_target_pairs={{0,15},{1,2},{2,1},{3,4},{4,3},{5,6},{6,5},{7,8},{8,7},{9,10},{10,... | collective-permute-start | bytes 1769480 | tf_op jit(solution)/shard_map/ppermute | solution.py:536
  12.1 26.1 %copy-start = (bf16[128,128]{1,0:T(8,128)(2,1)S(1)}, bf16[128,128]{1,0:T(8,128)(2,1)}, u32[]{:S(2)}) copy-start(bf16[128,128]{1,0:T(8,128)(2,1)} %constant.13.clone.dz) | copy-start | bytes 98308
  12.1 26.0 %copy-start.1 = (bf16[64,192]{1,0:T(8,128)(2,1)S(1)}, bf16[64,192]{1,0:T(8,128)(2,1)}, u32[]{:S(2)}) copy-start(bf16[64,192]{1,0:T(8,128)(2,1)} %constant.12.clone.dy3) | copy-start | bytes 73732
  34.0 4.1 %collective-permute-start.2 = (f32[3,8,128]{2,1,0:T(8,128)S(1)}, f32[3,8,128]{2,1,0:T(8,128)S(1)}, u32[]{:S(2)}, u32[]{:S(2)}) collective-permute-start(f32[3,8,128]{2,1,0:T(8,128)S(1)} %pad_maximum_fusion.mine), channel_id=1, source_target_pairs={{0,1},{1,0},{2,3},{3,2},{4,5},{5,4},{6,7},{7,6},{8,9},{9,8},{10,11... | collective-permute-start | bytes 36872 | tf_op jit(solution)/shard_map/ppermute | solution.py:543

commit v6 on v5

--- a/solution.py
+++ b/solution.py
@@ -18,7 +18,6 @@
 LEFT = ITERS
 RIGHT = ITERS + 1
 TALL = LEFT + ROWS + RIGHT
-LOAD_UNROLL = 4
 CHUNK = 8
 ROOM = 24 * 1024 * 1024
 NY = 64
@@ -168,21 +167,18 @@
     return [r for r in spans if len(r)]
 
 
-def write_marks(lev, coef, marks):
+def write_marks(lev, marks):
     level_x, level_y, level_z = lev[0, 0], lev[0, 1], lev[0, 2]
-    weight = coef[0].astype(jnp.float32)
     lane = lax.broadcasted_iota(jnp.int32, (8, 128), 1)
     groups_y = lax.shift_left(1, level_y - LOW)
     width_z = lax.shift_left(1, level_z)
     for b, (plane, group, source, width, _, _) in enumerate(BLOCKS):
         keep = (lane >= source) & (lane < jnp.minimum(width_z, source + width)) & (group < groups_y) & (level_x >= NEED[plane])
-        kept = jnp.where(keep, 1.0, 0.0)
-        marks[b] = kept
-        marks[len(BLOCKS) + b] = weight * kept
-    marks[2 * len(BLOCKS)] = jnp.full((8, 128), parity() * 1.0, jnp.float32)
-
-
-def inner_kernel(lev_h, coef, den, kap, hy3, hz, f_ref, c_ref, cl_ref, old_l, old_r, ends, marks, hy3_v, hz_v, den_v, kap_v, lev, sem, sem_w):
+        marks[b] = jnp.where(keep, 1.0, 0.0)
+    marks[len(BLOCKS)] = jnp.full((8, 128), parity() * 1.0, jnp.float32)
+
+
+def inner_kernel(lev_h, den, kap, hy3, hz, f_ref, c_ref, cl_ref, old_l, old_r, ends, marks, hy3_v, hz_v, den_v, kap_v, lev, sem, sem_w):
     parts = ROWS // CHUNK
 
     def copies(part):
@@ -197,26 +193,28 @@
             copy.start()
     weights = [pltpu.make_async_copy(hy3, hy3_v, sem_w.at[0]), pltpu.make_async_copy(hz, hz_v, sem_w.at[1])]
     scalars = [pltpu.make_async_copy(lev_h, lev, sem_w.at[2])]
-    for copy in weights + scalars:
+    for copy in scalars + weights:
         copy.start()
-    before = jnp.zeros((8, 8, 128), jnp.float32)
+    for copy in scalars:
+        copy.wait()
+    write_marks(lev, marks)
     for part in range(parts):
         for copy in copies(part):
             copy.wait()
 
-        def load(t, before):
-            for u in range(LOAD_UNROLL):
-                i = part * CHUNK + t * LOAD_UNROLL + u
+        @pl.when(parity() < 2)
+        def _(part=part):
+            before = fetch(kap_v, part * CHUNK - 1) if part else None
+            for i in range(part * CHUNK, part * CHUNK + CHUNK):
                 k = fetch(kap_v, i)
                 f_ref[i] = fetch(den_v, i)
-                c_ref[0, jnp.maximum(i - 1, 0)] = 0.5 * (before + k)
+                if before is not None:
+                    c_ref[0, i - 1] = 0.5 * (before + k)
                 c_ref[1, i], c_ref[2, i], c_ref[3, i], c_ref[4, i], cl_ref[i] = row_coefs(k)
                 before = k
-            return before
-
-        before = lax.fori_loop(0, CHUNK // LOAD_UNROLL, load, before)
+
     ends[0] = fetch(kap_v, 0)
-    ends[1] = before
+    ends[1] = fetch(kap_v, ROWS - 1)
 
     for step in range(1, ITERS + 1):
         for rows in inner_rows(step):
@@ -231,9 +229,6 @@
 
             step_rows(rows, lambda i: f_ref[i], put, lambda a, i: c_ref[a, i], lambda i: cl_ref[i], keep)
     old_r[ITERS - 1] = f_ref[ROWS - 1 - ITERS]
-    for copy in scalars:
-        copy.wait()
-    write_marks(lev, coef, marks)
     for copy in weights:
         copy.wait()
 
@@ -243,23 +238,8 @@
     out[...] = lanes_dot(jnp.concatenate(planes, axis=0), hz[...]).reshape(out.shape)
 
 
-def one_end(is_left, state, halo, f_new, c_new, cl_new):
-    f_in, c_in, cl_in, old_l, old_r, ends = state
-    fresh = set()
-
-    def take(i):
-        return f_new[i + LEFT] if i in fresh or not 0 <= i < ROWS else f_in[i]
-
-    def put(i, value):
-        fresh.add(i)
-        f_new[i + LEFT] = value
-
-    def coef_at(a, i):
-        return c_in[a, i] if 0 <= i < ROWS - 1 or (a and i == ROWS - 1) else c_new[a, i + LEFT]
-
-    def first_y(i):
-        return cl_in[i] if 0 <= i < ROWS else cl_new[i + LEFT]
-
+def read_end(is_left, state, halo, f_new, c_new, cl_new):
+    ends = state[5]
     skip = RIGHT - LEFT if is_left else 0
     first, count = (-LEFT, LEFT) if is_left else (ROWS, RIGHT)
     before = None if is_left else ends[1]
@@ -274,6 +254,25 @@
     if is_left:
         c_new[0, LEFT - 1] = 0.5 * (before + ends[0])
 
+
+def one_end(is_left, state, halo, f_new, c_new, cl_new):
+    read_end(is_left, state, halo, f_new, c_new, cl_new)
+    f_in, c_in, cl_in, old_l, old_r, _ = state
+    fresh = set()
+
+    def take(i):
+        return f_new[i + LEFT] if i in fresh or not 0 <= i < ROWS else f_in[i]
+
+    def put(i, value):
+        fresh.add(i)
+        f_new[i + LEFT] = value
+
+    def coef_at(a, i):
+        return c_in[a, i] if 0 <= i < ROWS - 1 or (a and i == ROWS - 1) else c_new[a, i + LEFT]
+
+    def first_y(i):
+        return cl_in[i] if 0 <= i < ROWS else cl_new[i + LEFT]
+
     for step in range(1, ITERS + 1):
         reach = ITERS - step
         if is_left:
@@ -308,7 +307,8 @@
 
 
 def cross_kernel(*refs):
-    state, (marks, hy3, hz, near, halo, out, stay), work, nodes, nodal = refs[:6], refs[6:13], refs[13:16], refs[16], refs[17]
+    state, (marks, hy3, hz, near, halo, coef, out, stay) = refs[:6], refs[6:14]
+    work, nodes, nodal = refs[14:17], refs[17], refs[18]
     for n in (1, 2):
         nodes[n] = state[0][n * GAP]
 
@@ -326,11 +326,11 @@
         nodes[4] = take(4 * GAP)
 
     hierarchize([nodes[n] for n in range(NODES)], hy3, hz, nodal)
-    finish(marks, nodal, out, stay)
-
-
-def finish(marks, nodal, out, stay):
-    swapped = marks[2 * len(BLOCKS)] > 0.5
+    finish(coef, marks, nodal, out, stay)
+
+
+def finish(coef, marks, nodal, out, stay):
+    swapped = marks[len(BLOCKS)] > 0.5
 
     def planes_of(group):
         u = [nodal[n, group] for n in range(NODES)]
@@ -349,8 +349,10 @@
     for b, (plane, group, source, width, tile, first) in enumerate(BLOCKS):
         if group not in cache:
             cache[group] = planes_of(group)
-        value = marks[len(BLOCKS) + b] * cache[group][plane]
+        value = marks[b] * cache[group][plane]
         tiles[tile] = tiles[tile] + shifted(value, first - source)
+    weight = jnp.broadcast_to(coef[...].astype(jnp.float32), (8, 128))
+    tiles = [weight * tile for tile in tiles]
     for member in range(out.shape[0]):
         out[member] = tiles[0]
     for tile in range(1, TILES):
@@ -358,7 +360,7 @@
 
 
 def spread_kernel(marks, mine, other, dy3, dz, out, held, sem):
-    swapped = marks[2 * len(BLOCKS), 0:1] > 0.5
+    swapped = marks[len(BLOCKS), 0:1] > 0.5
     zero = jnp.zeros((8, 128), jnp.float32)
     planes = [[zero] * 8 for _ in range(5)]
     outer_other = [zero] * 8
@@ -443,7 +445,7 @@
     )(far(den), far(kap))
 
 
-def inner(levels, coefs, den, kap, interpret=False):
+def inner(levels, den, kap, interpret=False):
     rows = rows_shape(ROWS)
     hy3, hz, _, _ = constants()
     return pl.pallas_call(
@@ -455,11 +457,11 @@
             rows_shape(4),
             rows_shape(ITERS),
             rows_shape(2),
-            jax.ShapeDtypeStruct((2 * len(BLOCKS) + 1, 8, 128), jnp.float32),
+            jax.ShapeDtypeStruct((len(BLOCKS) + 1, 8, 128), jnp.float32),
             jax.ShapeDtypeStruct(hy3.shape, jnp.bfloat16),
             jax.ShapeDtypeStruct(hz.shape, jnp.bfloat16),
         ),
-        in_specs=[FAR, SMEM] + [FAR] * 4,
+        in_specs=[FAR] * 5,
         out_specs=(VMEM,) * 9,
         scratch_shapes=[pltpu.VMEM((ROWS, NY, NZ), jnp.float32)] * 2
         + [
@@ -471,7 +473,7 @@
         cost_estimate=pl.CostEstimate(flops=20_000_000, bytes_accessed=8_000_000, transcendentals=0),
         interpret=interpret,
         name="inner",
-    )(far(levels), coefs, far(den), far(kap), far(jnp.asarray(hy3, jnp.bfloat16)), far(jnp.asarray(hz, jnp.bfloat16)))
+    )(far(levels), far(den), far(kap), far(jnp.asarray(hy3, jnp.bfloat16)), far(jnp.asarray(hz, jnp.bfloat16)))
 
 
 def work():
@@ -496,20 +498,20 @@
     )(*state[:6], halo)
 
 
-def cross_end(members, state, near, halo, interpret=False):
+def cross_end(members, coefs, state, near, halo, interpret=False):
     return pl.pallas_call(
         cross_kernel,
         out_shape=(
             jax.ShapeDtypeStruct((members, 8, 128), jnp.float32),
             jax.ShapeDtypeStruct((TILES - 1, 8, 128), jnp.float32),
         ),
-        in_specs=[VMEM] * 11,
+        in_specs=[VMEM] * 12,
         out_specs=(VMEM, VMEM),
         scratch_shapes=work() + [pltpu.VMEM((NODES, 8, 8, 128), jnp.float32)] * 2,
         compiler_params=params(),
         interpret=interpret,
         name="cross_end",
-    )(*state, near, halo)
+    )(*state, near, halo, coefs.reshape(1, 1))
 
 
 def spread(marks, mine, other, interpret=False):
@@ -535,9 +537,9 @@
     to_cross, to_chip = send(den, kap)
     cross = lax.ppermute(to_cross, "space", other_chip)
     chip = lax.ppermute(to_chip, "space", pair)
-    state = inner(levels, coefs, den, kap)
+    state = inner(levels, den, kap)
     near = chip_end(state, chip)
-    sent, stay = cross_end(grid, state, near, cross)
+    sent, stay = cross_end(grid, coefs, state, near, cross)
     got = lax.all_to_all(sent, "grid", split_axis=0, concat_axis=0, tiled=True)
     mine = jnp.concatenate([jnp.sum(got, axis=0, keepdims=True), stay], axis=0)
     other = lax.ppermute(mine, "space", pair)

time: 39.8 us -> 39.8 us (level)
  waiting for transfers between devices: 2.87 us -> 3.32 us
  Pallas kernels: 11.4 us -> 11 us
    pallas_call x1, Pallas kernels: 5.63 us -> 5.17 us  [inner(): pl.pallas_call(inner_kernel, out_shape=(rows, rows_shape(5, ROWS), jax.Sh...]
    ppermute x1, waiting for transfers between devices: 2.03 us -> 2.48 us  [local(): cross = lax.ppermute(to_cross, 'space', other_chip)]
  transfers between devices with their start and end apart: 3 -> 3, of which waited for: 2 -> 2; matrix products, arithmetic and copies ran while one was open for 0% -> 0% of each run, Pallas kernels for 17% -> 16%
where the time goes in v6:
time: 39.8 us; the launch traced here: 39.7 us
  blocking collectives  18 us (45%)
  Pallas kernels  11 us (28%)
  starting transfers between devices  6.6 us (17%)
  waiting for transfers between devices  3.32 us (8%)
  between operations  0.71 us (2%)
    all_to_all x1, blocking collectives, local(): got = lax.all_to_all(sent, 'grid', split_axis=0, concat_axis=0, tiled=True)  18 us
    pallas_call x1, Pallas kernels, inner(): pl.pallas_call(inner_kernel, out_shape=(rows, rows_shape(5, ROWS), jax.Sh...  5.17 us
    ppermute x1, starting transfers between devices, local(): other = lax.ppermute(mine, 'space', pair)  3.31 us
    ppermute x1, starting transfers between devices, local(): chip = lax.ppermute(to_chip, 'space', pair)  3.29 us
    ppermute x1, waiting for transfers between devices, local(): cross = lax.ppermute(to_cross, 'space', other_chip)  2.48 us
    pallas_call x1, Pallas kernels, cross_end(): pl.pallas_call(cross_kernel, out_shape=(jax.ShapeDtypeStruct((members, 8,...  1.85 us
    pallas_call x1, Pallas kernels, spread(): pl.pallas_call(spread_kernel, out_shape=jax.ShapeDtypeStruct((ROWS, NY, N...  1.46 us
    pallas_call x1, Pallas kernels, send(): pl.pallas_call(send_kernel, out_shape=(jax.ShapeDtypeStruct((2 * RIGHT, N...  1.26 us
  transfers between devices with their start and end apart: 3, of which 2 were waited for; matrix products, arithmetic and copies ran while one was open for 0% of the time, Pallas kernels for 16%

profile of v6, /device:TPU:1, one launch (start us, length us, event | category | flops | bytes accessed | tf_op | source)
XLA Modules:
  0.0 39.7 jit_solution(8088345400605880125)
XLA Ops:
  0.0 1.3 %send.1 = (f32[18,64,128]{2,1,0:T(8,128)S(1)}, f32[18,64,128]{2,1,0:T(8,128)S(1)}) custom-call(f32[32,64,128]{2,1,0:T(8,128)} %bitcast.6, f32[32,64,128]{2,1,0:T(8,128)} %bitcast.8), custom_call_target="tpu_custom_call" | custom-call | tf_op jit(solution)/shard_map/send/pallas_call | solution.py:433
  1.3 3.3 %collective-permute-start = (f32[18,64,128]{2,1,0:T(8,128)S(1)}, f32[18,64,128]{2,1,0:T(8,128)S(1)}, u32[]{:S(2)}, u32[]{:S(2)}) collective-permute-start(f32[18,64,128]{2,1,0:T(8,128)S(1)} %get-tuple-element.27), channel_id=1, source_target_pairs={{0,1},{1,0},{2,3},{3,2},{4,5},{5,4},{6,7},{7,6},{8,9},{9,8},{10,11... | collective-permute-start | bytes 1769480 | tf_op jit(solution)/shard_map/ppermute | solution.py:539
  4.6 0.0 collective-permute-start.1
  5.2 5.2 %inner.1 = (f32[32,8,8,128]{3,2,1,0:T(8,128)S(1)}, f32[5,32,8,8,128]{4,3,2,1,0:T(8,128)S(1)}, f32[32,8,128]{2,1,0:T(8,128)S(1)}, f32[4,8,8,128]{3,2,1,0:T(8,128)...) custom-call(s32[1,3]{1,0:T(1,128)} %lev_h.1, ...), custom_call_target="tpu_custom_call" | custom-call | flops 20000000 | bytes 8000000 | tf_op jit(solution)/shard_map/inner/pallas_call | solution.py:451
  10.4 0.0 collective-permute-done.refs_6_
  10.4 1.2 %chip_end.1.refs_9_ = f32[2,8,8,128]{3,2,1,0:T(8,128)S(1)} custom-call(f32[32,8,8,128]{3,2,1,0:T(8,128)S(1)} %get-tuple-element.19.refs_0_, f32[5,32,8,8,128]{4,3,2,1,0:T(8,128)S(1)} %get-tuple-element.20.refs_1_, f32[32,8,128]{2,1,0:T(8,128)S(1)} %get-tuple-element.21.refs_2_, f32[4,8,8,128]{3,2,1,0:T(8,128)S(1)} %get-tuple-element.22.refs_3_, ...), custom_call_target="tpu_custom_call" | custom-call | flops 10000000 | bytes 4000000 | tf_op jit(solution)/shard_map/chip_end/pallas_call | solution.py:488
  11.7 0.0 copy-start
  11.7 0.0 copy-start.1
  11.7 2.5 %collective-permute-done.1.refs_10_ = f32[18,64,128]{2,1,0:T(8,128)S(1)} collective-permute-done((f32[18,64,128]{2,1,0:T(8,128)S(1)}, f32[18,64,128]{2,1,0:T(8,128)S(1)}, u32[]{:S(2)}, u32[]{:S(2)}) %collective-permute-start.1) | collective-permute-done | bytes 589856 | tf_op jit(solution)/shard_map/ppermute | solution.py:538
  14.2 1.9 %cross_end.1 = (f32[16,8,128]{2,1,0:T(8,128)S(1)}, f32[2,8,128]{2,1,0:T(8,128)S(1)}) custom-call(f32[32,8,8,128]{3,2,1,0:T(8,128)S(1)} %get-tuple-element.19.refs_0_, f32[5,32,8,8,128]{4,3,2,1,0:T(8,128)S(1)} %get-tuple-element.20.refs_1_, f32[32,8,128]{2,1,0:T(8,128)S(1)} %get-tuple-element.21.refs_2_, f32[4,8,8,128]{3,2,1,0:T(8,128)S(1)} %get-tuple-element.22.refs_3_, ...), custom_call_target="tpu_custom_call" | custom-call | tf_op jit(solution)/shard_map/cross_end/pallas_call | solution.py:502
  16.0 18.0 %all_to_all.5 = f32[16,8,128]{2,1,0:T(8,128)S(1)} all-to-all(f32[16,8,128]{2,1,0:T(8,128)S(1)} %get-tuple-element.29), channel_id=1, replica_groups=mesh['grid'=16,'space'=16] {'grid'}, dimensions={0} | all-to-all | bytes 131072 | tf_op jit(solution)/shard_map/all_to_all | solution.py:543
  34.1 3.3 %collective-permute-start.2 = (f32[3,8,128]{2,1,0:T(8,128)S(1)}, f32[3,8,128]{2,1,0:T(8,128)S(1)}, u32[]{:S(2)}, u32[]{:S(2)}) collective-permute-start(f32[3,8,128]{2,1,0:T(8,128)S(1)} %pad_maximum_fusion.mine), channel_id=1, source_target_pairs={{0,1},{1,0},{2,3},{3,2},{4,5},{5,4},{6,7},{7,6},{8,9},{9,8},{10,11... | collective-permute-start | bytes 36872 | tf_op jit(solution)/shard_map/ppermute | solution.py:545
  37.4 0.8 %collective-permute-done.2.other = f32[3,8,128]{2,1,0:T(8,128)S(1)} collective-permute-done((f32[3,8,128]{2,1,0:T(8,128)S(1)}, f32[3,8,128]{2,1,0:T(8,128)S(1)}, u32[]{:S(2)}, u32[]{:S(2)}) %collective-permute-start.2) | collective-permute-done | bytes 12320 | tf_op jit(solution)/shard_map/ppermute | solution.py:545
  38.2 0.0 copy-done
  38.2 0.0 copy-done.1
  38.2 1.5 %spread.1 = f32[32,64,128]{2,1,0:T(8,128)} custom-call(f32[24,8,128]{2,1,0:T(8,128)S(1)} %get-tuple-element.18.refs_6_.marks, f32[3,8,128]{2,1,0:T(8,128)S(1)} %pad_maximum_fusion.mine, f32[3,8,128]{2,1,0:T(8,128)S(1)} %collective-permute-done.2.other, bf16[64,192]{1,0:T(8,128)(2,1)S(1)} %copy-done.1, bf16[128,128]{1,0:T(8,128)(2,1)S(1)} %copy-done), custom_call_target="tpu_custom_call" | custom-call | tf_op jit(solution)/shard_map/spread/pallas_call | solution.py:519
  (2 shorter events, 0.0 us)
Async XLA Ops:
  1.3 9.1 %collective-permute-start = (f32[18,64,128]{2,1,0:T(8,128)S(1)}, f32[18,64,128]{2,1,0:T(8,128)S(1)}, u32[]{:S(2)}, u32[]{:S(2)}) collective-permute-start(f32[18,64,128]{2,1,0:T(8,128)S(1)} %get-tuple-element.27), channel_id=1, source_target_pairs={{0,1},{1,0},{2,3},{3,2},{4,5},{5,4},{6,7},{7,6},{8,9},{9,8},{10,11... | collective-permute-start | bytes 1769480 | tf_op jit(solution)/shard_map/ppermute | solution.py:539
  4.6 9.6 %collective-permute-start.1 = (f32[18,64,128]{2,1,0:T(8,128)S(1)}, f32[18,64,128]{2,1,0:T(8,128)S(1)}, u32[]{:S(2)}, u32[]{:S(2)}) collective-permute-start(f32[18,64,128]{2,1,0:T(8,128)S(1)} %get-tuple-element.28), channel_id=1, source_target_pairs={{0,15},{1,2},{2,1},{3,4},{4,3},{5,6},{6,5},{7,8},{8,7},{9,10},{10,... | collective-permute-start | bytes 1769480 | tf_op jit(solution)/shard_map/ppermute | solution.py:538
  11.7 26.5 %copy-start = (bf16[128,128]{1,0:T(8,128)(2,1)S(1)}, bf16[128,128]{1,0:T(8,128)(2,1)}, u32[]{:S(2)}) copy-start(bf16[128,128]{1,0:T(8,128)(2,1)} %constant.13.clone.dz) | copy-start | bytes 98308
  11.7 26.5 %copy-start.1 = (bf16[64,192]{1,0:T(8,128)(2,1)S(1)}, bf16[64,192]{1,0:T(8,128)(2,1)}, u32[]{:S(2)}) copy-start(bf16[64,192]{1,0:T(8,128)(2,1)} %constant.12.clone.dy3) | copy-start | bytes 73732
  34.1 4.1 %collective-permute-start.2 = (f32[3,8,128]{2,1,0:T(8,128)S(1)}, f32[3,8,128]{2,1,0:T(8,128)S(1)}, u32[]{:S(2)}, u32[]{:S(2)}) collective-permute-start(f32[3,8,128]{2,1,0:T(8,128)S(1)} %pad_maximum_fusion.mine), channel_id=1, source_target_pairs={{0,1},{1,0},{2,3},{3,2},{4,5},{5,4},{6,7},{7,6},{8,9},{9,8},{10,11... | collective-permute-start | bytes 36872 | tf_op jit(solution)/shard_map/ppermute | solution.py:545

commit v7 on v6

--- a/solution.py
+++ b/solution.py
@@ -16,8 +16,9 @@
 GAP = 8
 NODES = ROWS // GAP + 1
 LEFT = ITERS
-RIGHT = ITERS + 1
-TALL = LEFT + ROWS + RIGHT
+RIGHT = ITERS
+TALL = LEFT + ROWS + RIGHT + 1
+SENT = 2 * ITERS + 1
 CHUNK = 8
 ROOM = 24 * 1024 * 1024
 NY = 64
@@ -240,19 +241,21 @@
 
 def read_end(is_left, state, halo, f_new, c_new, cl_new):
     ends = state[5]
-    skip = RIGHT - LEFT if is_left else 0
-    first, count = (-LEFT, LEFT) if is_left else (ROWS, RIGHT)
+    first = -LEFT if is_left else ROWS
     before = None if is_left else ends[1]
-    for t in range(count):
+    for t in range(ITERS):
         at = first + t + LEFT
-        k = fetch(halo, RIGHT + skip + t)
-        f_new[at] = fetch(halo, skip + t)
+        k = fetch(halo, ITERS + t)
+        f_new[at] = fetch(halo, t)
         c_new[1, at], c_new[2, at], c_new[3, at], c_new[4, at], cl_new[at] = row_coefs(k)
         if before is not None:
             c_new[0, at - 1] = 0.5 * (before + k)
         before = k
     if is_left:
         c_new[0, LEFT - 1] = 0.5 * (before + ends[0])
+    else:
+        f_new[TALL - 1] = f_new[TALL - 2]
+        c_new[0, TALL - 2] = jnp.zeros_like(before)
 
 
 def one_end(is_left, state, halo, f_new, c_new, cl_new):
@@ -299,7 +302,7 @@
     def _():
         take = one_end(False, state, halo, *work)
         out[0] = take(3 * GAP)
-        out[1] = take(4 * GAP)
+        out[1] = take(4 * GAP) + fetch(halo, SENT - 1)
 
     @pl.when(parity() == 1)
     def _():
@@ -323,7 +326,7 @@
         take = one_end(False, state, halo, *work)
         nodes[0] = near[0]
         nodes[3] = take(3 * GAP)
-        nodes[4] = take(4 * GAP)
+        nodes[4] = take(4 * GAP) + fetch(halo, SENT - 1)
 
     hierarchize([nodes[n] for n in range(NODES)], hy3, hz, nodal)
     finish(coef, marks, nodal, out, stay)
@@ -403,18 +406,28 @@
 FAR = pl.BlockSpec(memory_space=pltpu.HBM)
 
 
-def send_kernel(den, kap, cross, chip, sem):
-    low = (ROWS - RIGHT) * parity()
+def straight(halo, far):
+    part = halo[ITERS - 1]
+    part = far[0] - part
+    for j in range(ITERS):
+        after = halo[ITERS + j + 1] if j < ITERS - 1 else far[1]
+        part = part * (0.5 * (halo[ITERS + j] + after))
+    return part
+
+
+def send_kernel(low_core, den, kap, out, far, sem):
+    start = jnp.where(parity() == low_core, 0, ROWS - ITERS)
     copies = []
-    for n, (out, start) in enumerate(((cross, low), (chip, ROWS - RIGHT - low))):
-        for m, source in enumerate((den, kap)):
-            copies.append(
-                pltpu.make_async_copy(source.at[pl.ds(start, RIGHT)], out.at[pl.ds(m * RIGHT, RIGHT)], sem.at[n, m])
-            )
+    for m, source in enumerate((den, kap)):
+        copies.append(
+            pltpu.make_async_copy(source.at[pl.ds(start, ITERS)], out.at[pl.ds(m * ITERS, ITERS)], sem.at[m])
+        )
+        copies.append(pltpu.make_async_copy(source.at[ITERS], far.at[m], sem.at[2 + m]))
     for copy in copies:
         copy.start()
     for copy in copies:
         copy.wait()
+    out[SENT - 1] = straight(out, far)
 
 
 def params(room=ROOM):
@@ -429,16 +442,13 @@
     return pltpu.with_memory_space_constraint(x, pltpu.HBM)
 
 
-def send(den, kap, interpret=False):
+def send(low_core, den, kap, interpret=False):
     return pl.pallas_call(
-        send_kernel,
-        out_shape=(
-            jax.ShapeDtypeStruct((2 * RIGHT, NY, NZ), jnp.float32),
-            jax.ShapeDtypeStruct((2 * RIGHT, NY, NZ), jnp.float32),
-        ),
+        functools.partial(send_kernel, low_core),
+        out_shape=jax.ShapeDtypeStruct((SENT, NY, NZ), jnp.float32),
         in_specs=[FAR] * 2,
-        out_specs=(VMEM, VMEM),
-        scratch_shapes=[pltpu.SemaphoreType.DMA((2, 2))],
+        out_specs=VMEM,
+        scratch_shapes=[pltpu.VMEM((2, NY, NZ), jnp.float32), pltpu.SemaphoreType.DMA((4,))],
         compiler_params=params(8 * 1024 * 1024),
         interpret=interpret,
         name="send",
@@ -534,9 +544,8 @@
     assert den.shape == (ROWS, NY, NZ) and space * ROWS == 512
     pair = [(i, i ^ 1) for i in range(space)]
     other_chip = [(i, (i + 1 if i % 2 else i - 1) % space) for i in range(space)]
-    to_cross, to_chip = send(den, kap)
-    cross = lax.ppermute(to_cross, "space", other_chip)
-    chip = lax.ppermute(to_chip, "space", pair)
+    cross = lax.ppermute(send(0, den, kap), "space", other_chip)
+    chip = lax.ppermute(send(1, den, kap), "space", pair)
     state = inner(levels, den, kap)
     near = chip_end(state, chip)
     sent, stay = cross_end(grid, coefs, state, near, cross)

time: 39.8 us -> 40.5 us (1.018)
  Pallas kernels: 11 us -> 12 us
    pallas_call x1 -> x2, Pallas kernels: 1.26 us -> 2.23 us  [send(): pl.pallas_call(functools.partial(send_kernel, low_core), out_shape=jax.Sh...]
where the time goes in v7:
time: 40.5 us; the launch traced here: 40.3 us
  blocking collectives  18 us (44%)
  Pallas kernels  12 us (30%)
  starting transfers between devices  6.62 us (16%)
  waiting for transfers between devices  2.96 us (7%)
  between operations  0.72 us (2%)
    all_to_all x1, blocking collectives, local(): got = lax.all_to_all(sent, 'grid', split_axis=0, concat_axis=0, tiled=True)  18 us
    pallas_call x1, Pallas kernels, inner(): pl.pallas_call(inner_kernel, out_shape=(rows, rows_shape(5, ROWS), jax.Sh...  5.17 us
    ppermute x1, starting transfers between devices, local(): chip = lax.ppermute(send(1, den, kap), 'space', pair)  3.29 us
    ppermute x1, starting transfers between devices, local(): other = lax.ppermute(mine, 'space', pair)  3.24 us
    pallas_call x2, Pallas kernels, send(): pl.pallas_call(functools.partial(send_kernel, low_core), out_shape=jax.Sh...  2.23 us
    ppermute x1, waiting for transfers between devices, local(): cross = lax.ppermute(send(0, den, kap), 'space', other_chip)  2.12 us
    pallas_call x1, Pallas kernels, cross_end(): pl.pallas_call(cross_kernel, out_shape=(jax.ShapeDtypeStruct((members, 8,...  1.87 us
    pallas_call x1, Pallas kernels, spread(): pl.pallas_call(spread_kernel, out_shape=jax.ShapeDtypeStruct((ROWS, NY, N...  1.46 us
  transfers between devices with their start and end apart: 3, of which 2 were waited for; matrix products, arithmetic and copies ran while one was open for 0% of the time, Pallas kernels for 16%

profile of v7, /device:TPU:1, one launch (start us, length us, event | category | flops | bytes accessed | tf_op | source)
XLA Modules:
  0.0 40.3 jit_solution(10866190653204134983)
XLA Ops:
  0.0 1.1 %send.2 = f32[17,64,128]{2,1,0:T(8,128)S(1)} custom-call(f32[32,64,128]{2,1,0:T(8,128)} %bitcast.6, f32[32,64,128]{2,1,0:T(8,128)} %bitcast.9), custom_call_target="tpu_custom_call" | custom-call | tf_op jit(solution)/shard_map/send/pallas_call | solution.py:446
  1.1 3.3 %collective-permute-start = (f32[17,64,128]{2,1,0:T(8,128)S(1)}, f32[17,64,128]{2,1,0:T(8,128)S(1)}, u32[]{:S(2)}, u32[]{:S(2)}) collective-permute-start(f32[17,64,128]{2,1,0:T(8,128)S(1)} %send.2), channel_id=1, source_target_pairs={{0,1},{1,0},{2,3},{3,2},{4,5},{5,4},{6,7},{7,6},{8,9},{9,8},{10,11... | collective-permute-start | bytes 1671176 | tf_op jit(solution)/shard_map/ppermute | solution.py:548
  4.4 1.1 %send.3 = f32[17,64,128]{2,1,0:T(8,128)S(1)} custom-call(f32[32,64,128]{2,1,0:T(8,128)} %bitcast.7, f32[32,64,128]{2,1,0:T(8,128)} %bitcast.10), custom_call_target="tpu_custom_call" | custom-call | tf_op jit(solution)/shard_map/send/pallas_call | solution.py:446
  5.5 0.1 collective-permute-start.1
  6.3 5.2 %inner.1 = (f32[32,8,8,128]{3,2,1,0:T(8,128)S(1)}, f32[5,32,8,8,128]{4,3,2,1,0:T(8,128)S(1)}, f32[32,8,128]{2,1,0:T(8,128)S(1)}, f32[4,8,8,128]{3,2,1,0:T(8,128)...) custom-call(s32[1,3]{1,0:T(1,128)} %lev_h.1, ...), custom_call_target="tpu_custom_call" | custom-call | flops 20000000 | bytes 8000000 | tf_op jit(solution)/shard_map/inner/pallas_call | solution.py:461
  11.5 0.0 collective-permute-done.refs_6_
  11.5 1.2 %chip_end.1.refs_9_ = f32[2,8,8,128]{3,2,1,0:T(8,128)S(1)} custom-call(f32[32,8,8,128]{3,2,1,0:T(8,128)S(1)} %get-tuple-element.17.refs_0_, f32[5,32,8,8,128]{4,3,2,1,0:T(8,128)S(1)} %get-tuple-element.18.refs_1_, f32[32,8,128]{2,1,0:T(8,128)S(1)} %get-tuple-element.19.refs_2_, f32[4,8,8,128]{3,2,1,0:T(8,128)S(1)} %get-tuple-element.20.refs_3_, ...), custom_call_target="tpu_custom_call" | custom-call | flops 10000000 | bytes 4000000 | tf_op jit(solution)/shard_map/chip_end/pallas_call | solution.py:498
  12.7 0.0 copy-start
  12.7 0.0 copy-start.1
  12.8 2.1 %collective-permute-done.1.refs_10_ = f32[17,64,128]{2,1,0:T(8,128)S(1)} collective-permute-done((f32[17,64,128]{2,1,0:T(8,128)S(1)}, f32[17,64,128]{2,1,0:T(8,128)S(1)}, u32[]{:S(2)}, u32[]{:S(2)}) %collective-permute-start.1) | collective-permute-done | bytes 557088 | tf_op jit(solution)/shard_map/ppermute | solution.py:547
  14.9 1.9 %cross_end.1 = (f32[16,8,128]{2,1,0:T(8,128)S(1)}, f32[2,8,128]{2,1,0:T(8,128)S(1)}) custom-call(f32[32,8,8,128]{3,2,1,0:T(8,128)S(1)} %get-tuple-element.17.refs_0_, f32[5,32,8,8,128]{4,3,2,1,0:T(8,128)S(1)} %get-tuple-element.18.refs_1_, f32[32,8,128]{2,1,0:T(8,128)S(1)} %get-tuple-element.19.refs_2_, f32[4,8,8,128]{3,2,1,0:T(8,128)S(1)} %get-tuple-element.20.refs_3_, ...), custom_call_target="tpu_custom_call" | custom-call | tf_op jit(solution)/shard_map/cross_end/pallas_call | solution.py:512
  16.8 18.0 %all_to_all.5 = f32[16,8,128]{2,1,0:T(8,128)S(1)} all-to-all(f32[16,8,128]{2,1,0:T(8,128)S(1)} %get-tuple-element.25), channel_id=1, replica_groups=mesh['grid'=16,'space'=16] {'grid'}, dimensions={0} | all-to-all | bytes 131072 | tf_op jit(solution)/shard_map/all_to_all | solution.py:552
  34.8 3.2 %collective-permute-start.2 = (f32[3,8,128]{2,1,0:T(8,128)S(1)}, f32[3,8,128]{2,1,0:T(8,128)S(1)}, u32[]{:S(2)}, u32[]{:S(2)}) collective-permute-start(f32[3,8,128]{2,1,0:T(8,128)S(1)} %pad_maximum_fusion.mine), channel_id=1, source_target_pairs={{0,1},{1,0},{2,3},{3,2},{4,5},{5,4},{6,7},{7,6},{8,9},{9,8},{10,11... | collective-permute-start | bytes 36872 | tf_op jit(solution)/shard_map/ppermute | solution.py:554
  38.0 0.8 %collective-permute-done.2.other = f32[3,8,128]{2,1,0:T(8,128)S(1)} collective-permute-done((f32[3,8,128]{2,1,0:T(8,128)S(1)}, f32[3,8,128]{2,1,0:T(8,128)S(1)}, u32[]{:S(2)}, u32[]{:S(2)}) %collective-permute-start.2) | collective-permute-done | bytes 12320 | tf_op jit(solution)/shard_map/ppermute | solution.py:554
  38.8 0.0 copy-done
  38.8 0.0 copy-done.1
  38.8 1.5 %spread.1 = f32[32,64,128]{2,1,0:T(8,128)} custom-call(f32[24,8,128]{2,1,0:T(8,128)S(1)} %get-tuple-element.16.refs_6_.marks, f32[3,8,128]{2,1,0:T(8,128)S(1)} %pad_maximum_fusion.mine, f32[3,8,128]{2,1,0:T(8,128)S(1)} %collective-permute-done.2.other, bf16[64,192]{1,0:T(8,128)(2,1)S(1)} %copy-done.1, bf16[128,128]{1,0:T(8,128)(2,1)S(1)} %copy-done), custom_call_target="tpu_custom_call" | custom-call | tf_op jit(solution)/shard_map/spread/pallas_call | solution.py:529
  (2 shorter events, 0.0 us)
Async XLA Ops:
  1.1 10.3 %collective-permute-start = (f32[17,64,128]{2,1,0:T(8,128)S(1)}, f32[17,64,128]{2,1,0:T(8,128)S(1)}, u32[]{:S(2)}, u32[]{:S(2)}) collective-permute-start(f32[17,64,128]{2,1,0:T(8,128)S(1)} %send.2), channel_id=1, source_target_pairs={{0,1},{1,0},{2,3},{3,2},{4,5},{5,4},{6,7},{7,6},{8,9},{9,8},{10,11... | collective-permute-start | bytes 1671176 | tf_op jit(solution)/shard_map/ppermute | solution.py:548
  5.5 9.3 %collective-permute-start.1 = (f32[17,64,128]{2,1,0:T(8,128)S(1)}, f32[17,64,128]{2,1,0:T(8,128)S(1)}, u32[]{:S(2)}, u32[]{:S(2)}) collective-permute-start(f32[17,64,128]{2,1,0:T(8,128)S(1)} %send.3), channel_id=1, source_target_pairs={{0,15},{1,2},{2,1},{3,4},{4,3},{5,6},{6,5},{7,8},{8,7},{9,10},{10,... | collective-permute-start | bytes 1671176 | tf_op jit(solution)/shard_map/ppermute | solution.py:547
  12.7 26.1 %copy-start = (bf16[128,128]{1,0:T(8,128)(2,1)S(1)}, bf16[128,128]{1,0:T(8,128)(2,1)}, u32[]{:S(2)}) copy-start(bf16[128,128]{1,0:T(8,128)(2,1)} %constant.13.clone.dz) | copy-start | bytes 98308
  12.7 26.1 %copy-start.1 = (bf16[64,192]{1,0:T(8,128)(2,1)S(1)}, bf16[64,192]{1,0:T(8,128)(2,1)}, u32[]{:S(2)}) copy-start(bf16[64,192]{1,0:T(8,128)(2,1)} %constant.12.clone.dy3) | copy-start | bytes 73732
  34.8 4.1 %collective-permute-start.2 = (f32[3,8,128]{2,1,0:T(8,128)S(1)}, f32[3,8,128]{2,1,0:T(8,128)S(1)}, u32[]{:S(2)}, u32[]{:S(2)}) collective-permute-start(f32[3,8,128]{2,1,0:T(8,128)S(1)} %pad_maximum_fusion.mine), channel_id=1, source_target_pairs={{0,1},{1,0},{2,3},{3,2},{4,5},{5,4},{6,7},{7,6},{8,9},{9,8},{10,11... | collective-permute-start | bytes 36872 | tf_op jit(solution)/shard_map/ppermute | solution.py:554
